TPU v7x, 32 devices: a whole 2x2x4 slice. The times are simulated.
32 devices in a mesh: dp: 4 (over x, core), blk: 4 (over z), ulysses: 2 (over y).
Axes of the slice: x: 2, y: 2, z: 4, core: 2. Of those that a mesh axis runs over, the one named last changes fastest.
Arguments:
- tokens: bfloat16 [8192, 768], P(('dp', 'blk', 'ulysses')), may hold values from -6 to 6
- cotangent: bfloat16 [8192, 768], P(('dp', 'blk', 'ulysses')), may hold values from -6 to 6
- lengths: int32 [4], P('dp'), may hold values from 512 to 2048, as said below
- stretch_order: int32 [8], replicated, may hold values from 0 to 7, each once
- gain_attn: bfloat16 [768], P(('dp', 'blk', 'ulysses')), may hold values from 0.5 to 1.5
- w_query: bfloat16 [768, 768], P(('dp', 'blk', 'ulysses')), may hold values from -0.21875 to 0.21875
- w_key: bfloat16 [768, 768], P(('dp', 'blk', 'ulysses')), may hold values from -0.21875 to 0.21875
- w_value: bfloat16 [768, 768], P(('dp', 'blk', 'ulysses')), may hold values from -0.21875 to 0.21875
- w_out: bfloat16 [768, 768], P(('dp', 'blk', 'ulysses')), may hold values from -3 to 3
- gain_ffn: bfloat16 [768], P(('dp', 'blk', 'ulysses')), may hold values from 0.5 to 1.5
- w_gate: bfloat16 [768, 2048], P(('dp', 'blk', 'ulysses')), may hold values from -0.21875 to 0.21875
- w_up: bfloat16 [768, 2048], P(('dp', 'blk', 'ulysses')), may hold values from -0.21875 to 0.21875
- w_down: bfloat16 [768, 2048], P(('dp', 'blk', 'ulysses')), may hold values from -0.5 to 0.5
Outputs:
- output: float32 [8192, 768], P(('dp', 'blk', 'ulysses'))
- grad_input: float32 [8192, 768], P(('dp', 'blk', 'ulysses'))
- grad_gain_attn: float32 [768], P(('dp', 'blk', 'ulysses'))
- grad_w_query: float32 [768, 768], P(('dp', 'blk', 'ulysses'))
- grad_w_key: float32 [768, 768], P(('dp', 'blk', 'ulysses'))
- grad_w_value: float32 [768, 768], P(('dp', 'blk', 'ulysses'))
- grad_w_out: float32 [768, 768], P(('dp', 'blk', 'ulysses'))
- grad_gain_ffn: float32 [768], P(('dp', 'blk', 'ulysses'))
- grad_w_gate: float32 [768, 2048], P(('dp', 'blk', 'ulysses'))
- grad_w_up: float32 [768, 2048], P(('dp', 'blk', 'ulysses'))
- grad_w_down: float32 [768, 2048], P(('dp', 'blk', 'ulysses'))
Inputs may be any that keep to these rules, and one draw needn't show every extreme that they name: `lengths`: one sequence has all 2048 slots live and another 2048 // 4 in every draw. Each stretch number once; storage block j of every sequence holds its positions stretch_order[j] * 256 onward.
All inputs are finite; a program needn't handle non-finite values.
Results may differ from a plain program's by a relative error of at most 0.017.
Values may be sent and summed in bfloat16 or wider, within the bound.
No kernel may reach another device: no remote copies, remote signals or barrier semaphores. Data moves between devices by JAX's collectives and lax.ppermute only.
A program may use at most 128 MiB of HBM per device.

v0:
```python
import functools
import math

import jax
import jax.numpy as jnp
from jax import lax
from jax.experimental import pallas as pl
from jax.experimental.pallas import tpu as pltpu
from jax.sharding import PartitionSpec as P


HEADS = 12
HEAD_DIM = 64

BRANCH_SCALE = 1.4 / math.sqrt(40.0)
NORM_EPS = 1e-05
MASKED = -1e30
SCORE_SCALE = HEAD_DIM ** (-0.5)

ALL = ("dp", "blk", "ulysses")
F32 = jnp.float32
BF16 = jnp.bfloat16


def after(value, *earlier):
    return lax.optimization_barrier((value,) + earlier)[0]


def normalize(values):
    inverse = lax.rsqrt(jnp.mean(values * values, axis=-1, keepdims=True) + NORM_EPS)
    return (values * inverse, inverse)


def norm_back(d_scaled, scaled, inverse):
    return inverse * (d_scaled - scaled * jnp.mean(d_scaled * scaled, axis=-1, keepdims=True))


def dot(left, right, left_dim, right_dim):
    return lax.dot_general(
        left, right, (((left_dim,), (right_dim,)), ((), ())), preferred_element_type=F32
    )


def in_order(flag, mine, other, axis):
    first = jnp.where(flag == 0, mine, other)
    second = jnp.where(flag == 0, other, mine)
    return jnp.stack([first, second], axis=axis)


def roll_to(pieces, shift):
    count = pieces.shape[0]
    doubled = jnp.concatenate([pieces, pieces], axis=0)
    return lax.dynamic_slice_in_dim(doubled, shift, count, 0)


def allowed_block(key_stretch, query_stretch, length, rows):
    key_pos = key_stretch * rows + lax.broadcasted_iota(jnp.int32, (rows, rows), 0)
    query_pos = query_stretch * rows + lax.broadcasted_iota(jnp.int32, (rows, rows), 1)
    return (key_pos <= query_pos) & (key_pos < length)


def flip2(value):
    return jnp.transpose(value)


def forward_kernel(own_count, other_count, group, rows, stretch_ref, length_ref, *refs):
    key_count = own_count + other_count
    queries, refs = refs[:own_count], refs[own_count:]
    keys, refs = refs[:key_count], refs[key_count:]
    outs, refs = refs[:own_count], refs[own_count:]
    exact_ref, logsum_ref, q_s, k_s, v_s, out_s, top_s, total_s, accum_s = refs
    width = group * HEAD_DIM
    for block in range(key_count):
        if block < own_count:
            q_s[block] = queries[block][...]
        for head in range(group):
            at = head * HEAD_DIM
            k_s[block, head] = flip2(keys[block][at : at + HEAD_DIM, :])
        v_s[block] = keys[block][width:, :]
    length = length_ref[0]

    def step(query_block, key_block, masked):
        if masked:
            allowed = allowed_block(
                stretch_ref[key_block], stretch_ref[query_block], length, rows
            )
        heads = range(group)
        spans = [slice(head * HEAD_DIM, (head + 1) * HEAD_DIM) for head in heads]
        scores = [
            jnp.dot(
                k_s[key_block, head], q_s[query_block, spans[head], :], preferred_element_type=F32
            )
            for head in heads
        ]
        tops, totals = top_s[...], total_s[...]
        new_tops, new_totals, products, fades = [], [], [], []
        for head in heads:
            score = jnp.where(allowed, scores[head], MASKED) if masked else scores[head]
            top = tops[head : head + 1, :]
            top_new = jnp.maximum(top, jnp.max(score, axis=0, keepdims=True))
            weights = jnp.exp(score - top_new)
            if masked:
                weights = jnp.where(allowed, weights, 0.0)
            fade = jnp.exp(top - top_new)
            new_tops.append(top_new)
            new_totals.append(
                totals[head : head + 1, :] * fade + jnp.sum(weights, axis=0, keepdims=True)
            )
            fades.append(fade)
            products.append(
                jnp.dot(
                    v_s[key_block, spans[head], :],
                    weights.astype(BF16),
                    preferred_element_type=F32,
                )
            )
        for head in heads:
            top_s[head : head + 1, :] = new_tops[head]
            total_s[head : head + 1, :] = new_totals[head]
            accum_s[spans[head], :] = accum_s[spans[head], :] * fades[head] + products[head]

    def over_queries(query_block, carry):
        top_s[...] = jnp.full(top_s.shape, MASKED, F32)
        total_s[...] = jnp.zeros(total_s.shape, F32)
        accum_s[...] = jnp.zeros(accum_s.shape, F32)
        mine = stretch_ref[query_block]

        def over_keys(key_block, inner):
            theirs = stretch_ref[key_block]
            active = (theirs <= mine) & (theirs * rows < length)
            partial = (theirs == mine) | (theirs * rows + rows > length)

            @pl.when(active & jnp.logical_not(partial))
            def _():
                step(query_block, key_block, False)

            @pl.when(active & partial)
            def _():
                step(query_block, key_block, True)

            return inner

        lax.fori_loop(0, key_count, over_keys, 0)
        for head in range(group):
            at = head * HEAD_DIM
            total = total_s[head : head + 1, :]
            value = accum_s[at : at + HEAD_DIM, :] / total
            exact_ref[query_block, at : at + HEAD_DIM, :] = value
            out_s[query_block, at : at + HEAD_DIM, :] = value.astype(BF16)
        logsum_ref[query_block] = top_s[...] + jnp.log(total_s[...])
        return carry

    lax.fori_loop(0, own_count, over_queries, 0)
    for block in range(own_count):
        outs[block][...] = out_s[block]


def backward_kernel(own_count, other_count, group, rows, stretch_ref, length_ref, *refs):
    key_count = own_count + other_count
    queries, refs = refs[:own_count], refs[own_count:]
    keys, refs = refs[:key_count], refs[key_count:]
    douts, refs = refs[:own_count], refs[own_count:]
    (exact_ref, logsum_ref), refs = refs[:2], refs[2:]
    dq_outs, refs = refs[:own_count], refs[own_count:]
    dkv_outs, refs = refs[:key_count], refs[key_count:]
    q_s, k_s, kt_s, v_s, do_s, delta_s, dq_s, dkv_s = refs
    width = group * HEAD_DIM
    for block in range(key_count):
        if block < own_count:
            q_s[block] = queries[block][...]
            do_s[block] = douts[block][...]
            product = douts[block][...].astype(F32) * exact_ref[block]
            for head in range(group):
                at = head * HEAD_DIM
                delta_s[block, head : head + 1, :] = jnp.sum(
                    product[at : at + HEAD_DIM, :], axis=0, keepdims=True
                )
        kt_s[block] = keys[block][:width, :]
        for head in range(group):
            at = head * HEAD_DIM
            k_s[block, head] = flip2(keys[block][at : at + HEAD_DIM, :])
            v_s[block, head] = flip2(keys[block][at + width : at + width + HEAD_DIM, :])
    dq_s[...] = jnp.zeros(dq_s.shape, F32)
    dkv_s[...] = jnp.zeros(dkv_s.shape, F32)
    length = length_ref[0]

    def step(query_block, key_block, masked):
        if masked:
            allowed = allowed_block(
                stretch_ref[key_block], stretch_ref[query_block], length, rows
            )
        heads = range(group)
        spans = [slice(head * HEAD_DIM, (head + 1) * HEAD_DIM) for head in heads]
        q_t = [q_s[query_block, span, :] for span in spans]
        do_t = [do_s[query_block, span, :] for span in spans]
        scores = [
            jnp.dot(k_s[key_block, head], q_t[head], preferred_element_type=F32) for head in heads
        ]
        d_attends = [
            jnp.dot(v_s[key_block, head], do_t[head], preferred_element_type=F32) for head in heads
        ]
        logsums, deltas = logsum_ref[query_block], delta_s[query_block]
        dks, dvs, dqs = [], [], []
        for head in heads:
            attend = jnp.exp(scores[head] - logsums[head : head + 1, :])
            if masked:
                attend = jnp.where(allowed, attend, 0.0)
            d_scores = (attend * (d_attends[head] - deltas[head : head + 1, :])).astype(BF16)
            dvs.append(dot(do_t[head], attend.astype(BF16), 1, 1))
            dks.append(dot(q_t[head], d_scores, 1, 1))
            dqs.append(
                jnp.dot(kt_s[key_block, spans[head], :], d_scores, preferred_element_type=F32)
            )
        dkv_s[key_block] += jnp.concatenate(dks + dvs, axis=0)
        dq_s[query_block] += jnp.concatenate(dqs, axis=0)

    def over_queries(query_block, carry):
        mine = stretch_ref[query_block]

        def over_keys(key_block, inner):
            theirs = stretch_ref[key_block]
            live = mine * rows < length

            @pl.when(live & (theirs < mine))
            def _():
                step(query_block, key_block, False)

            @pl.when(live & (theirs == mine))
            def _():
                step(query_block, key_block, True)

            return inner

        return lax.fori_loop(0, key_count, over_keys, carry)

    lax.fori_loop(0, own_count, over_queries, 0)
    for block in range(own_count):
        dq_outs[block][...] = (dq_s[block] * SCORE_SCALE).astype(BF16)
    for block in range(key_count):
        dkv_outs[block][...] = dkv_s[block].astype(dkv_outs[block].dtype)


def in_smem():
    return pl.BlockSpec(memory_space=pltpu.SMEM)


def in_vmem():
    return pl.BlockSpec(memory_space=pltpu.VMEM)


def attention_forward(stretches, length, queries, keys, group):
    rows = queries[0].shape[1]
    width = group * HEAD_DIM
    count, blocks = len(queries), len(keys)
    outs = pl.pallas_call(
        functools.partial(forward_kernel, count, blocks - count, group, rows),
        out_shape=(jax.ShapeDtypeStruct((width, rows), BF16),) * count
        + (
            jax.ShapeDtypeStruct((count, width, rows), F32),
            jax.ShapeDtypeStruct((count, 8, rows), F32),
        ),
        in_specs=[in_smem()] * 2 + [in_vmem()] * (count + blocks),
        out_specs=(in_vmem(),) * (count + 2),
        scratch_shapes=[
            pltpu.VMEM((count, width, rows), BF16),
            pltpu.VMEM((blocks, group, rows, HEAD_DIM), BF16),
            pltpu.VMEM((blocks, width, rows), BF16),
            pltpu.VMEM((count, width, rows), BF16),
            pltpu.VMEM((8, rows), F32),
            pltpu.VMEM((8, rows), F32),
            pltpu.VMEM((width, rows), F32),
        ],
        name="attention_forward",
    )(stretches, length, *queries, *keys)
    return outs[:count], outs[count], outs[count + 1]


def attention_backward(stretches, length, queries, keys, douts, exact, logsum, group):
    rows = queries[0].shape[1]
    width = group * HEAD_DIM
    count, blocks = len(queries), len(keys)
    outs = pl.pallas_call(
        functools.partial(backward_kernel, count, blocks - count, group, rows),
        out_shape=(jax.ShapeDtypeStruct((width, rows), BF16),) * count
        + (jax.ShapeDtypeStruct((2 * width, rows), F32),) * count
        + (jax.ShapeDtypeStruct((2 * width, rows), BF16),) * (blocks - count),
        in_specs=[in_smem()] * 2 + [in_vmem()] * (2 * count + blocks + 2),
        out_specs=(in_vmem(),) * (count + blocks),
        scratch_shapes=[
            pltpu.VMEM((count, width, rows), BF16),
            pltpu.VMEM((blocks, group, rows, HEAD_DIM), BF16),
            pltpu.VMEM((blocks, width, rows), BF16),
            pltpu.VMEM((blocks, group, rows, HEAD_DIM), BF16),
            pltpu.VMEM((count, width, rows), BF16),
            pltpu.VMEM((count, 8, rows), F32),
            pltpu.VMEM((count, width, rows), F32),
            pltpu.VMEM((blocks, 2 * width, rows), F32),
        ],
        name="attention_backward",
    )(stretches, length, *queries, *keys, *douts, exact, logsum)
    return outs[:count], outs[count:]


def local(
    tokens,
    cotangent,
    lengths,
    stretch_order,
    gain_attn,
    w_query,
    w_key,
    w_value,
    w_out,
    gain_ffn,
    w_gate,
    w_up,
    w_down,
):
    rows, width = tokens.shape
    hidden_units = w_gate.shape[1]
    shard = w_query.shape[0]
    blk_size = lax.axis_size("blk")
    uly_size = lax.axis_size("ulysses")
    dp_size = lax.axis_size("dp")
    assert dp_size == 4 and uly_size == 2
    head_parts = math.gcd(HEADS, blk_size)
    group = HEADS // head_parts
    part_width = group * HEAD_DIM
    members = (blk_size // head_parts) * uly_size
    stretch_count = stretch_order.shape[0]
    assert stretch_count == blk_size * uly_size

    dp_at = lax.axis_index("dp")
    blk_at = lax.axis_index("blk")
    uly_at = lax.axis_index("ulysses")
    x_at, core_at = dp_at // 2, dp_at % 2
    part_at = blk_at % head_parts
    member_at = (blk_at // head_parts) * uly_size + uly_at

    def over_core(value):
        return lax.ppermute(value, "dp", [(i, i ^ 1) for i in range(dp_size)])

    def over_x(value):
        return lax.ppermute(value, "dp", [(i, i ^ 2) for i in range(dp_size)])

    def over_y(value):
        return lax.ppermute(value, "ulysses", [(i, i ^ 1) for i in range(uly_size)])

    def over_blk(value, shift):
        return lax.ppermute(value, "blk", [(i, (i + shift) % blk_size) for i in range(blk_size)])

    def over_part(value, shift):
        return lax.ppermute(
            value,
            "blk",
            [
                (i, i - i % head_parts + (i + shift) % head_parts)
                for i in range(blk_size)
            ],
        )

    def over_member(value, shift):
        pairs = []
        for source in range(blk_size * uly_size):
            blk, uly = divmod(source, uly_size)
            member = (blk // head_parts) * uly_size + uly
            target = (member + shift) % members
            new_blk = (target // uly_size) * head_parts + blk % head_parts
            pairs.append((source, new_blk * uly_size + target % uly_size))
        return lax.ppermute(value, ("blk", "ulysses"), pairs)

    labels = jnp.arange(stretch_count, dtype=jnp.int32)
    places = []
    for member_shift in range(members):
        for part_shift in range(head_parts):
            member = (member_at - member_shift) % members
            part = (part_at - part_shift) % head_parts
            block = (member // uly_size) * head_parts + part
            places.append(block * uly_size + member % uly_size)
    places = jnp.stack(places).astype(jnp.int32)
    stretches = jnp.sum(
        jnp.where(places[:, None] == labels[None, :], stretch_order[None, :], 0), axis=1
    ).astype(jnp.int32)
    length = lengths[0]

    own_pos = stretches[0] * rows + jnp.arange(rows, dtype=jnp.int32)
    half_dim = HEAD_DIM // 2
    freqs = jnp.exp(jnp.arange(half_dim, dtype=F32) * (-2.0 * math.log(10000.0) / HEAD_DIM))
    angles = freqs[:, None] * own_pos.astype(F32)[None, :]
    cosine, sine_part = jnp.cos(angles), jnp.sin(angles)

    def rotate(values, direction):
        first = values[..., :half_dim, :]
        second = values[..., half_dim:, :]
        return jnp.concatenate(
            [
                first * cosine - direction * second * sine_part,
                second * cosine + direction * first * sine_part,
            ],
            axis=-2,
        )

    def plane_first(first, second):
        return over_x(first), over_y(second), over_x(second)

    def plane_second(first, second, first_x, second_y, second_x):
        second_xy = over_x(second_y)
        first_y = over_y(first)
        first_xy = over_y(first_x)
        return (
            plane(first, first_x, first_y, first_xy),
            plane(second, second_x, second_y, second_xy),
        )

    def plane(mine, by_x, by_y, by_xy):
        return in_order(
            x_at, in_order(uly_at, mine, by_y, 1), in_order(uly_at, by_x, by_xy, 1), 0
        )

    def from_line(piece):
        return [piece] + [over_blk(piece, shift) for shift in range(1, blk_size)]

    def line(arrived):
        backwards = jnp.stack([arrived[(-i) % blk_size] for i in range(blk_size)])
        return roll_to(backwards, (blk_size - blk_at) % blk_size)

    def both_cores(half):
        whole = jnp.broadcast_to(half[:, None], half.shape[:1] + (2,) + half.shape[1:])
        start = (0, 1 - core_at) + (0,) * (half.ndim - 1)
        whole = lax.dynamic_update_slice(whole, over_core(half)[:, None], start)
        return whole.reshape(width, -1)

    def by_part(part):
        span = slice(part * part_width, (part + 1) * part_width)
        return [w_key[:, span], w_value[:, span]]

    gains = jnp.pad(jnp.stack([gain_attn, gain_ffn], axis=1), ((0, 0), (0, 126)))
    qkv_local = jnp.concatenate(
        [gains, w_query] + [w for part in range(head_parts) for w in by_part(part)], axis=1
    )
    qkv_line = line(from_line(qkv_local))
    first_columns = 128 + 3 * width // 2
    qkv_halves = lax.optimization_barrier(
        (qkv_line[..., :first_columns], qkv_line[..., first_columns:])
    )
    qkv_firsts = plane_first(*qkv_halves)
    qkv_planes = plane_second(*qkv_halves, *qkv_firsts)
    qkv_half = jnp.concatenate(qkv_planes, axis=-1)
    qkv_all = both_cores(lax.optimization_barrier(qkv_half))
    gain_attn_all = qkv_all[:, 0].astype(F32)
    gain_ffn_all = qkv_all[:, 1].astype(F32)
    w_qkv = qkv_all[:, 128:]

    rest_local = jnp.concatenate([w_down, w_out, w_gate, w_up], axis=1)
    rest_arrived = from_line(after(rest_local, qkv_halves[0]))

    def pick(values, index, axis):
        return lax.dynamic_index_in_dim(values, index, axis, keepdims=False)

    def by_core(left_t):
        grid = left_t.reshape(2, 2, width // 4, rows)
        return tuple(
            pick(grid, core, 1).reshape(width // 2, rows) for core in (1 - core_at, core_at)
        )

    live = (own_pos < length).astype(F32)
    d_out = cotangent.astype(F32) * live[:, None]
    d_down = (BRANCH_SCALE * d_out).astype(BF16)
    inputs = tokens.astype(F32)
    scaled_in, inverse_in = normalize(inputs)
    normed_attn = (scaled_in * gain_attn_all[None, :]).astype(BF16)
    qkv_lin = dot(w_qkv, normed_attn, 0, 1)
    q_lin = qkv_lin[:width].reshape(head_parts, group, HEAD_DIM, rows)
    kv_lin = qkv_lin[width:].reshape(head_parts, 2, group, HEAD_DIM, rows)
    q_send = (rotate(q_lin, 1.0).astype(BF16) * SCORE_SCALE).astype(BF16)
    kv_send = jnp.stack(
        [rotate(kv_lin[:, 0], 1.0).astype(BF16), kv_lin[:, 1].astype(BF16)], axis=1
    )

    def scatter_parts(pieces):
        result = []
        for shift in range(head_parts):
            piece = lax.dynamic_index_in_dim(
                pieces, (part_at + shift) % head_parts, 0, keepdims=False
            )
            result.append(over_part(piece, shift) if shift else piece)
        return result

    def return_parts(pieces, *earlier):
        back = [
            after(over_part(piece, head_parts - shift), *earlier) if shift else piece
            for shift, piece in enumerate(pieces)
        ]
        return roll_to(jnp.stack(back), (head_parts - part_at) % head_parts)

    keys = scatter_parts(kv_send.reshape(head_parts, 2 * part_width, rows))
    queries = scatter_parts(q_send.reshape(head_parts, part_width, rows))
    keys = keys + [
        over_member(piece, member_shift)
        for member_shift in range(1, members)
        for piece in keys
    ]

    rest_arrived = [after(piece, keys[0]) for piece in rest_arrived]
    rest_line = line(rest_arrived)
    rest_halves = lax.optimization_barrier(
        (rest_line[..., :hidden_units], rest_line[..., hidden_units:])
    )
    rest_firsts = plane_first(*rest_halves)
    rest_planes = plane_second(
        *(after(piece, keys[-1]) for piece in rest_halves),
        *(after(piece, keys[-1]) for piece in rest_firsts),
    )
    down_half, other_half = rest_planes

    d_down_rows, normed_rows, lengths = lax.optimization_barrier(
        (by_core(jnp.transpose(d_down)), by_core(jnp.transpose(normed_attn)), lengths)
    )
    outs, exact_t, logsum = attention_forward(stretches, lengths, queries, keys, group)
    down_all = both_cores(lax.optimization_barrier(down_half))
    other_all = both_cores(lax.optimization_barrier(other_half))
    out_all = other_all[:, :width]
    gate_up_all = other_all[:, width:]

    attn_t = return_parts(outs).reshape(width, rows)

    middle = inputs + BRANCH_SCALE * dot(attn_t, out_all, 0, 0)
    scaled_mid, inverse_mid = normalize(middle)
    normed_ffn = (scaled_mid * gain_ffn_all[None, :]).astype(BF16)
    gate_up = dot(normed_ffn, gate_up_all, 1, 0)
    gate_act = gate_up[:, :hidden_units]
    upward = gate_up[:, hidden_units:]
    sigma = jax.nn.sigmoid(gate_act)
    silu_act = gate_act * sigma
    hidden = (silu_act * upward).astype(BF16)
    output = middle + BRANCH_SCALE * dot(hidden, down_all, 1, 1)

    d_hidden = dot(d_down, down_all, 1, 0)
    d_gate = (d_hidden * upward * sigma * (1.0 + gate_act * (1.0 - sigma))).astype(BF16)
    d_up = (d_hidden * silu_act).astype(BF16)
    d_gate_up = jnp.concatenate([d_gate, d_up], axis=1)
    d_normed_ffn = dot(d_gate_up, gate_up_all, 1, 1)
    d_middle = d_out + norm_back(d_normed_ffn * gain_ffn_all[None, :], scaled_mid, inverse_mid)
    d_branch = (BRANCH_SCALE * d_middle).astype(BF16)
    d_attn_t = dot(out_all, d_branch, 1, 1).astype(BF16)
    douts = scatter_parts(d_attn_t.reshape(head_parts, part_width, rows))

    def both(mine, theirs):
        return (mine.astype(F32) + theirs.astype(F32)).astype(BF16)

    def core_sum(left_rows, product):
        far = product(left_rows[0]).astype(BF16)
        near = product(left_rows[1])
        arrived = over_core(far)
        return both(near, arrived).reshape(2, blk_size, 2, shard, -1)

    def x_sum(values, *earlier):
        arrived = over_x(pick(values, 1 - x_at, 0))
        return both(pick(values, x_at, 0), after(arrived, *earlier))

    def y_sum(values, axis, *earlier):
        arrived = over_y(pick(values, 1 - uly_at, axis))
        return both(pick(values, uly_at, axis), after(arrived, *earlier))

    def line_sum(values, *earlier):
        total = pick(values, blk_at, 0).astype(F32)
        for shift in range(1, blk_size):
            piece = pick(values, (blk_at + shift) % blk_size, 0)
            total = total + after(over_blk(piece, shift), *earlier).astype(F32)
        return total

    down_core = core_sum(d_down_rows, lambda l: dot(l, hidden, 1, 0))
    gate_up_core = core_sum(by_core(jnp.transpose(normed_ffn)), lambda l: dot(l, d_gate_up, 1, 0))
    out_core = core_sum(by_core(attn_t), lambda l: dot(l, d_branch, 1, 0))

    dq, dkv = attention_backward(stretches, lengths, queries, keys, douts, exact_t, logsum, group)
    d_q = return_parts(dq).reshape(HEADS, HEAD_DIM, rows)
    d_q_t = rotate(d_q.astype(F32), -1.0).astype(BF16).reshape(width, rows)
    q_core = core_sum(normed_rows, lambda l: dot(l, d_q_t, 1, 1))
    back = []
    for shift in range(head_parts):
        total = dkv[shift]
        for member_shift in range(1, members):
            theirs = dkv[member_shift * head_parts + shift]
            total = total + over_member(theirs, members - member_shift).astype(F32)
        back.append(total.astype(BF16))
    d_kv = return_parts(back, q_core)
    q_x = x_sum(q_core)
    gate_x = x_sum(gate_up_core[..., :hidden_units], back[-1])
    up_y = y_sum(gate_up_core[..., hidden_units:], 2, dkv[0])
    gate_sum = y_sum(gate_x, 1, d_kv)
    up_sum = x_sum(up_y, back[-1])
    down_sum = x_sum(y_sum(down_core, 2, dkv[0]), back[-1])
    out_sum = y_sum(x_sum(out_core, back[-1]), 1, d_kv)
    d_kv = d_kv.reshape(head_parts, 2, group, HEAD_DIM, rows)
    d_kv_t = jnp.stack(
        [rotate(d_kv[:, 0].astype(F32), -1.0).astype(BF16), d_kv[:, 1]], axis=1
    ).reshape(2 * width, rows)

    kv_core = core_sum(normed_rows, lambda l: dot(l, d_kv_t, 1, 1))
    k_x = x_sum(kv_core[..., :width])
    v_y = y_sum(kv_core[..., width:], 2)
    q_sum = y_sum(q_x, 1)
    k_sum = y_sum(k_x, 1)
    v_sum = x_sum(v_y)

    rest_sum = line_sum(jnp.concatenate([down_sum, out_sum, gate_sum, up_sum], axis=-1), q_sum, k_sum, v_sum)
    qkv_sum = line_sum(jnp.concatenate([q_sum, k_sum, v_sum], axis=-1))

    d_normed = dot(d_q_t, w_qkv[:, :width], 0, 1) + dot(d_kv_t, w_qkv[:, width:], 0, 1)
    d_inputs = d_middle + norm_back(d_normed * gain_attn_all[None, :], scaled_in, inverse_in)

    grad_query = qkv_sum[:, :width]
    grad_kv = qkv_sum[:, width:].reshape(shard, head_parts, 2, part_width)
    grad_key = grad_kv[:, :, 0].reshape(shard, width)
    grad_value = grad_kv[:, :, 1].reshape(shard, width)
    grad_down = rest_sum[:, :hidden_units]
    grad_out = rest_sum[:, hidden_units : hidden_units + width]
    grad_gate = rest_sum[:, hidden_units + width : 2 * hidden_units + width]
    grad_up = rest_sum[:, 2 * hidden_units + width :]

    def gain_grad(gain, pairs):
        total = sum(jnp.sum(w.astype(F32) * grad, axis=1) for w, grad in pairs)
        return total / gain.astype(F32)

    return (
        output,
        d_inputs,
        gain_grad(gain_attn, [(w_query, grad_query), (w_key, grad_key), (w_value, grad_value)]),
        grad_query,
        grad_key,
        grad_value,
        grad_out,
        gain_grad(gain_ffn, [(w_gate, grad_gate), (w_up, grad_up)]),
        grad_gate,
        grad_up,
        grad_down,
    )


def solution(mesh):
    row, flat = P(ALL, None), P(ALL)
    in_specs = (row, row, P("dp"), P(), flat, row, row, row, row, flat, row, row, row)
    out_specs = (row, row, flat, row, row, row, row, flat, row, row, row)
    return jax.shard_map(local, mesh=mesh, in_specs=in_specs, out_specs=out_specs, check_vma=False)
```

profile of v0, /device:TPU:0, one launch (start us, length us, event | category | flops | bytes accessed | tf_op | source)
XLA Modules:
  0.0 407.3 jit_solution(6813144946022794383)
XLA Ops:
  4.1 5.1 %collective-permute-start = (bf16[24,2432]{1,0:T(8,128)(2,1)S(1)}, bf16[24,2432]{1,0:T(8,128)(2,1)S(1)}, u32[]{:S(2)}, u32[]{:S(2)}) collective-permute-start(bf16[24,2432]{1,0:T(8,128)(2,1)S(1)} %concatenate.188), channel_id=1, source_target_pairs={{0,6},{2,0},{4,2},{6,4},{1,7},{3,1},{5,3},{7,5},{8,14},{10,8},{12,... | collective-permute-start | bytes 350216 | tf_op jit(solution)/shard_map/ppermute | solution.py:350
  12.8 6.5 %collective-permute-done.1 = bf16[24,2432]{1,0:T(8,128)(2,1)S(1)} collective-permute-done((bf16[24,2432]{1,0:T(8,128)(2,1)S(1)}, bf16[24,2432]{1,0:T(8,128)(2,1)S(1)}, u32[]{:S(2)}, u32[]{:S(2)}) %collective-permute-start.1) | collective-permute-done | bytes 116768 | tf_op jit(solution)/shard_map/ppermute | solution.py:350
  23.6 4.2 %collective-permute-done.6 = bf16[4,24,1152]{2,1,0:T(8,128)(2,1)S(1)} collective-permute-done((bf16[4,24,1152]{2,1,0:T(8,128)(2,1)S(1)}, bf16[4,24,1152]{2,1,0:T(8,128)(2,1)S(1)}, u32[]{:S(2)}, u32[]{:S(2)}) %collective-permute-start.6) | collective-permute-done | bytes 221216 | tf_op jit(solution)/shard_map/ppermute | solution.py:347
  29.4 5.2 %collective-permute-done.4 = bf16[4,24,1280]{2,1,0:T(8,128)(2,1)S(1)} collective-permute-done((bf16[4,24,1280]{2,1,0:T(8,128)(2,1)S(1)}, bf16[4,24,1280]{2,1,0:T(8,128)(2,1)S(1)}, u32[]{:S(2)}, u32[]{:S(2)}) %collective-permute-start.4) | collective-permute-done | bytes 245792 | tf_op jit(solution)/shard_map/ppermute | solution.py:344
  37.8 3.1 collective-permute-done.5
  59.9 19.9 %collective-permute-done.24 = bf16[24,6912]{1,0:T(8,128)(2,1)S(1)} collective-permute-done((bf16[24,6912]{1,0:T(8,128)(2,1)S(1)}, bf16[24,6912]{1,0:T(8,128)(2,1)S(1)}, u32[]{:S(2)}, u32[]{:S(2)}) %collective-permute-start.24) | collective-permute-done | bytes 331808 | tf_op jit(solution)/shard_map/ppermute | solution.py:350
  84.8 4.7 %collective-permute-done.13.refs_5_ = bf16[384,256]{1,0:T(8,128)(2,1)} collective-permute-done((bf16[384,256]{1,0:T(8,128)(2,1)S(1)}, bf16[384,256]{1,0:T(8,128)(2,1)}, u32[]{:S(2)}, u32[]{:S(2)}) %collective-permute-start.13) | collective-permute-done | bytes 196640 | tf_op jit(solution)/shard_map/ppermute | solution.py:353
  89.5 6.7 %collective-permute-done.14.refs_6_ = bf16[384,256]{1,0:T(8,128)(2,1)S(1)} collective-permute-done((bf16[384,256]{1,0:T(8,128)(2,1)S(1)}, bf16[384,256]{1,0:T(8,128)(2,1)S(1)}, u32[]{:S(2)}, u32[]{:S(2)}) %collective-permute-start.14) | collective-permute-done | bytes 196640 | tf_op jit(solution)/shard_map/ppermute | solution.py:353
  103.1 10.3 %collective-permute-done.17.refs_9_ = bf16[384,256]{1,0:T(8,128)(2,1)} collective-permute-done((bf16[384,256]{1,0:T(8,128)(2,1)}, bf16[384,256]{1,0:T(8,128)(2,1)}, u32[]{:S(2)}, u32[]{:S(2)}) %collective-permute-start.17) | collective-permute-done | bytes 196640 | tf_op jit(solution)/shard_map/ppermute | solution.py:370
  117.6 2.9 collective-permute-done.19.refs_11_
  120.5 13.4 %attention_forward.1 = (bf16[192,256]{1,0:T(8,128)(2,1)}, bf16[192,256]{1,0:T(8,128)(2,1)}, bf16[192,256]{1,0:T(8,128)(2,1)}, bf16[192,256]{1,0:T(8,128)(2,1)}, ...) custom-call(s32[8]{0:T(128)} %copy-done.52, s32[1]{0:T(128)} %copy.203.length_ref, ...), custom_call_target="tpu_custom_call" | custom-call | tf_op jit(solution)/shard_map/attention_forward/pallas_call | solution.py:255
  136.9 3.3 collective-permute-start.21
  146.4 14.5 %collective-permute-done.28 = bf16[4,24,4864]{2,1,0:T(8,128)(2,1)S(1)} collective-permute-done((bf16[4,24,4864]{2,1,0:T(8,128)(2,1)}, bf16[4,24,4864]{2,1,0:T(8,128)(2,1)S(1)}, u32[]{:S(2)}, u32[]{:S(2)}) %collective-permute-start.28) | collective-permute-done | bytes 933920 | tf_op jit(solution)/shard_map/ppermute | solution.py:344
  166.1 5.6 %collective-permute-done.33 = bf16[2,4,2,24,2048]{4,3,1,2,0:T(8,128)(2,1)S(1)} collective-permute-done((bf16[2,4,2,24,2048]{4,3,1,2,0:T(8,128)(2,1)S(1)}, bf16[2,4,2,24,2048]{4,3,1,2,0:T(8,128)(2,1)S(1)}, u32[]{:S(2)}, u32[]{:S(2)}) %collective-permute-start.33) | collective-permute-done | bytes 1572896 | tf_op jit(solution)/shard_map/ppermute | solution.py:341
  207.2 16.8 %attention_backward.1 = (bf16[192,256]{1,0:T(8,128)(2,1)}, bf16[192,256]{1,0:T(8,128)(2,1)}, bf16[192,256]{1,0:T(8,128)(2,1)}, bf16[192,256]{1,0:T(8,128)(2,1)},...) custom-call(s32[8]{0:T(128)} %copy-done.52, ...), custom_call_target="tpu_custom_call" | custom-call | tf_op jit(solution)/shard_map/attention_backward/pallas_call | solution.py:282
  227.1 3.1 collective-permute-done.37
  230.8 6.2 %collective-permute-done.38 = bf16[192,256]{1,0:T(8,128)(2,1)S(1)} collective-permute-done((bf16[192,256]{1,0:T(8,128)(2,1)}, bf16[192,256]{1,0:T(8,128)(2,1)S(1)}, u32[]{:S(2)}, u32[]{:S(2)}) %collective-permute-start.38) | collective-permute-done | bytes 98336 | tf_op jit(solution)/shard_map/ppermute | solution.py:353
  237.0 6.6 %collective-permute-done.39 = bf16[192,256]{1,0:T(8,128)(2,1)S(1)} collective-permute-done((bf16[192,256]{1,0:T(8,128)(2,1)}, bf16[192,256]{1,0:T(8,128)(2,1)S(1)}, u32[]{:S(2)}, u32[]{:S(2)}) %collective-permute-start.39) | collective-permute-done | bytes 98336 | tf_op jit(solution)/shard_map/ppermute | solution.py:353
  261.6 4.3 %collective-permute-start.62 = (bf16[4,2,24,768]{3,2,0,1:T(8,128)(2,1)S(1)}, bf16[4,2,24,768]{3,2,0,1:T(8,128)(2,1)S(1)}, u32[]{:S(2)}, u32[]{:S(2)}) collective-permute-start(bf16[4,2,24,768]{3,2,0,1:T(8,128)(2,1)S(1)} %bitcast.388), channel_id=1, source_target_pairs={{0,16},{8,24},{16,0},{24,8},{1,17},{9,25},{17,1},{25,9},{2,18},{10... | collective-permute-start | bytes 884744 | tf_op jit(solution)/shard_map/ppermute | solution.py:344
  265.9 5.2 %collective-permute-done.45 = bf16[384,256]{1,0:T(8,128)(2,1)S(1)} collective-permute-done((bf16[384,256]{1,0:T(8,128)(2,1)S(1)}, bf16[384,256]{1,0:T(8,128)(2,1)S(1)}, u32[]{:S(2)}, u32[]{:S(2)}) %collective-permute-start.45) | collective-permute-done | bytes 196640 | tf_op jit(solution)/shard_map/ppermute | solution.py:353
  276.2 4.2 %collective-permute-start.48 = (bf16[4,2,24,768]{3,2,0,1:T(8,128)(2,1)S(1)}, bf16[4,2,24,768]{3,2,0,1:T(8,128)(2,1)S(1)}, u32[]{:S(2)}, u32[]{:S(2)}) collective-permute-start(bf16[4,2,24,768]{3,2,0,1:T(8,128)(2,1)S(1)} %bitcast.389), channel_id=1, source_target_pairs={{0,16},{8,24},{16,0},{24,8},{1,17},{9,25},{17,1},{25,9},{2,18},{10... | collective-permute-start | bytes 884744 | tf_op jit(solution)/shard_map/ppermute | solution.py:344
  283.4 3.1 collective-permute-done.63
  290.6 3.2 collective-permute-done.49
  300.4 6.1 %collective-permute-done.53 = bf16[2,4,24,768]{3,2,1,0:T(8,128)(2,1)S(1)} collective-permute-done((bf16[2,4,24,768]{3,2,1,0:T(8,128)(2,1)S(1)}, bf16[2,4,24,768]{3,2,1,0:T(8,128)(2,1)S(1)}, u32[]{:S(2)}, u32[]{:S(2)}) %collective-permute-start.53) | collective-permute-done | bytes 294944 | tf_op jit(solution)/shard_map/ppermute | solution.py:347
  310.1 13.0 %collective-permute-done.59 = bf16[2,4,24,2048]{3,2,1,0:T(8,128)(2,1)S(1)} collective-permute-done((bf16[2,4,24,2048]{3,2,1,0:T(8,128)(2,1)S(1)}, bf16[2,4,24,2048]{3,2,1,0:T(8,128)(2,1)S(1)}, u32[]{:S(2)}, u32[]{:S(2)}) %collective-permute-start.59) | collective-permute-done | bytes 786464 | tf_op jit(solution)/shard_map/ppermute | solution.py:347
  332.3 4.6 %collective-permute-done.56 = bf16[24,2304]{1,0:T(8,128)(2,1)S(1)} collective-permute-done((bf16[24,2304]{1,0:T(8,128)(2,1)S(1)}, bf16[24,2304]{1,0:T(8,128)(2,1)S(1)}, u32[]{:S(2)}, u32[]{:S(2)}) %collective-permute-start.56) | collective-permute-done | bytes 110624 | tf_op jit(solution)/shard_map/ppermute | solution.py:350
  349.7 9.6 %collective-permute-done.67 = bf16[2,4,24,2048]{3,2,1,0:T(8,128)(2,1)} collective-permute-done((bf16[2,4,24,2048]{3,2,1,0:T(8,128)(2,1)}, bf16[2,4,24,2048]{3,2,1,0:T(8,128)(2,1)}, u32[]{:S(2)}, u32[]{:S(2)}) %collective-permute-start.67) | collective-permute-done | bytes 786464 | tf_op jit(solution)/shard_map/ppermute | solution.py:347
  361.3 5.6 %collective-permute-done.65 = bf16[4,2,24,2048]{3,2,0,1:T(8,128)(2,1)S(1)} collective-permute-done((bf16[4,2,24,2048]{3,2,0,1:T(8,128)(2,1)S(1)}, bf16[4,2,24,2048]{3,2,0,1:T(8,128)(2,1)S(1)}, u32[]{:S(2)}, u32[]{:S(2)}) %collective-permute-start.65) | collective-permute-done | bytes 786464 | tf_op jit(solution)/shard_map/ppermute | solution.py:344
  367.3 3.8 collective-permute-done.68
  371.2 3.9 collective-permute-done.66
  380.9 3.8 collective-permute-done.71
  384.7 20.1 %collective-permute-done.70 = bf16[24,6912]{1,0:T(8,128)(2,1)S(1)} collective-permute-done((bf16[24,6912]{1,0:T(8,128)(2,1)S(1)}, bf16[24,6912]{1,0:T(8,128)(2,1)S(1)}, u32[]{:S(2)}, u32[]{:S(2)}) %collective-permute-start.70) | collective-permute-done | bytes 331808 | tf_op jit(solution)/shard_map/ppermute | solution.py:350
  (421 shorter events, 174.8 us)
Async XLA Ops:
  43.1 15.4 %collective-permute-start.23 = (bf16[24,6912]{1,0:T(8,128)(2,1)S(1)}, bf16[24,6912]{1,0:T(8,128)(2,1)S(1)}, u32[]{:S(2)}, u32[]{:S(2)}) collective-permute-start(bf16[24,6912]{1,0:T(8,128)(2,1)S(1)} %pad_maximum_fusion.22), channel_id=1, source_target_pairs={{0,6},{2,0},{4,2},{6,4},{1,7},{3,1},{5,3},{7,5},{8,14},{10,8},{12,... | collective-permute-start | bytes 995336 | tf_op jit(solution)/shard_map/ppermute | solution.py:350
  44.3 35.5 %collective-permute-start.24 = (bf16[24,6912]{1,0:T(8,128)(2,1)S(1)}, bf16[24,6912]{1,0:T(8,128)(2,1)S(1)}, u32[]{:S(2)}, u32[]{:S(2)}) collective-permute-start(bf16[24,6912]{1,0:T(8,128)(2,1)S(1)} %pad_maximum_fusion.22), channel_id=1, source_target_pairs={{0,4},{2,6},{4,0},{6,2},{1,5},{3,7},{5,1},{7,3},{8,12},{10,14},{12... | collective-permute-start | bytes 995336 | tf_op jit(solution)/shard_map/ppermute | solution.py:350
  45.6 34.2 %collective-permute-start.25 = (bf16[24,6912]{1,0:T(8,128)(2,1)S(1)}, bf16[24,6912]{1,0:T(8,128)(2,1)S(1)}, u32[]{:S(2)}, u32[]{:S(2)}) collective-permute-start(bf16[24,6912]{1,0:T(8,128)(2,1)S(1)} %pad_maximum_fusion.22), channel_id=1, source_target_pairs={{0,2},{2,4},{4,6},{6,0},{1,3},{3,5},{5,7},{7,1},{8,10},{10,12},{12... | collective-permute-start | bytes 995336 | tf_op jit(solution)/shard_map/ppermute | solution.py:350
  55.1 26.1 %collective-permute-start.10 = (bf16[192,256]{1,0:T(8,128)(2,1)S(1)}, bf16[192,256]{1,0:T(8,128)(2,1)S(1)}, u32[]{:S(2)}, u32[]{:S(2)}) collective-permute-start(bf16[192,256]{1,0:T(8,128)(2,1)S(1)} %get-tuple-element.197), channel_id=1, source_target_pairs={{0,2},{2,4},{4,6},{6,0},{1,3},{3,5},{5,7},{7,1},{8,10},{10,12},{12... | collective-permute-start | bytes 294920 | tf_op jit(solution)/shard_map/ppermute | solution.py:353
  55.3 26.6 %collective-permute-start.11 = (bf16[192,256]{1,0:T(8,128)(2,1)S(1)}, bf16[192,256]{1,0:T(8,128)(2,1)S(1)}, u32[]{:S(2)}, u32[]{:S(2)}) collective-permute-start(bf16[192,256]{1,0:T(8,128)(2,1)S(1)} %get-tuple-element.196), channel_id=1, source_target_pairs={{0,4},{2,6},{4,0},{6,2},{1,5},{3,7},{5,1},{7,3},{8,12},{10,14},{12... | collective-permute-start | bytes 294920 | tf_op jit(solution)/shard_map/ppermute | solution.py:353
  58.4 25.0 %collective-permute-start.12 = (bf16[192,256]{1,0:T(8,128)(2,1)S(1)}, bf16[192,256]{1,0:T(8,128)(2,1)S(1)}, u32[]{:S(2)}, u32[]{:S(2)}) collective-permute-start(bf16[192,256]{1,0:T(8,128)(2,1)S(1)} %get-tuple-element.195), channel_id=1, source_target_pairs={{0,6},{2,0},{4,2},{6,4},{1,7},{3,1},{5,3},{7,5},{8,14},{10,8},{12,... | collective-permute-start | bytes 294920 | tf_op jit(solution)/shard_map/ppermute | solution.py:353
  79.8 16.4 %collective-permute-start.14 = (bf16[384,256]{1,0:T(8,128)(2,1)S(1)}, bf16[384,256]{1,0:T(8,128)(2,1)S(1)}, u32[]{:S(2)}, u32[]{:S(2)}) collective-permute-start(bf16[384,256]{1,0:T(8,128)(2,1)S(1)} %get-tuple-element.164), channel_id=1, source_target_pairs={{0,4},{2,6},{4,0},{6,2},{1,5},{3,7},{5,1},{7,3},{8,12},{10,14},{12... | collective-permute-start | bytes 589832 | tf_op jit(solution)/shard_map/ppermute | solution.py:353
  81.2 21.3 %collective-permute-start.16 = (bf16[384,256]{1,0:T(8,128)(2,1)S(1)}, bf16[384,256]{1,0:T(8,128)(2,1)S(1)}, u32[]{:S(2)}, u32[]{:S(2)}) collective-permute-start(bf16[384,256]{1,0:T(8,128)(2,1)S(1)} %get-tuple-element.166.refs_4_), channel_id=1, source_target_pairs={{0,1},{1,0},{2,3},{3,2},{4,5},{5,4},{6,7},{7,6},{8,9},{9,8},{10,11... | collective-permute-start | bytes 589832 | tf_op jit(solution)/shard_map/ppermute | solution.py:370
  81.9 59.6 %collective-permute-start.27 = (bf16[4,24,4864]{2,1,0:T(8,128)(2,1)S(1)}, bf16[4,24,4864]{2,1,0:T(8,128)(2,1)}, u32[]{:S(2)}, u32[]{:S(2)}) collective-permute-start(bf16[4,24,4864]{2,1,0:T(8,128)(2,1)S(1)} %constant_dynamic-slice_fusion.16), channel_id=1, source_target_pairs={{0,16},{8,24},{16,0},{24,8},{1,17},{9,25},{17,1},{25,9},{2,18},{10... | collective-permute-start | bytes 2801672 | tf_op jit(solution)/shard_map/ppermute | solution.py:344
  83.4 59.5 %collective-permute-start.26 = (bf16[4,24,4864]{2,1,0:T(8,128)(2,1)S(1)}, bf16[4,24,4864]{2,1,0:T(8,128)(2,1)}, u32[]{:S(2)}, u32[]{:S(2)}) collective-permute-start(bf16[4,24,4864]{2,1,0:T(8,128)(2,1)S(1)} %constant_dynamic-slice_fusion.16), channel_id=1, source_target_pairs={{0,1},{1,0},{2,3},{3,2},{4,5},{5,4},{6,7},{7,6},{8,9},{9,8},{10,11... | collective-permute-start | bytes 2801672 | tf_op jit(solution)/shard_map/ppermute | solution.py:347
  96.9 16.5 %collective-permute-start.17 = (bf16[384,256]{1,0:T(8,128)(2,1)}, bf16[384,256]{1,0:T(8,128)(2,1)}, u32[]{:S(2)}, u32[]{:S(2)}) collective-permute-start(bf16[384,256]{1,0:T(8,128)(2,1)} %collective-permute-done.13.refs_5_), channel_id=1, source_target_pairs={{0,1},{1,0},{2,3},{3,2},{4,5},{5,4},{6,7},{7,6},{8,9},{9,8},{10,11... | collective-permute-start | bytes 589832 | tf_op jit(solution)/shard_map/ppermute | solution.py:370
  101.1 39.2 %collective-permute-start.31 = (bf16[4,24,2048]{2,1,0:T(8,128)(2,1)S(1)}, bf16[4,24,2048]{2,1,0:T(8,128)(2,1)}, u32[]{:S(2)}, u32[]{:S(2)}) collective-permute-start(bf16[4,24,2048]{2,1,0:T(8,128)(2,1)S(1)} %constant_dynamic-slice_fusion), channel_id=1, source_target_pairs={{0,16},{8,24},{16,0},{24,8},{1,17},{9,25},{17,1},{25,9},{2,18},{10... | collective-permute-start | bytes 1179656 | tf_op jit(solution)/shard_map/ppermute | solution.py:344
  136.9 28.1 %collective-permute-start.21 = (bf16[192,256]{1,0:T(8,128)(2,1)}, bf16[192,256]{1,0:T(8,128)(2,1)S(1)}, u32[]{:S(2)}, u32[]{:S(2)}) collective-permute-start(bf16[192,256]{1,0:T(8,128)(2,1)} %get-tuple-element.67), channel_id=1, source_target_pairs={{0,4},{2,6},{4,0},{6,2},{1,5},{3,7},{5,1},{7,3},{8,12},{10,14},{12... | collective-permute-start | bytes 294920 | tf_op jit(solution)/shard_map/ppermute | solution.py:353
  140.3 24.8 %collective-permute-start.22 = (bf16[192,256]{1,0:T(8,128)(2,1)}, bf16[192,256]{1,0:T(8,128)(2,1)S(1)}, u32[]{:S(2)}, u32[]{:S(2)}) collective-permute-start(bf16[192,256]{1,0:T(8,128)(2,1)} %get-tuple-element.68), channel_id=1, source_target_pairs={{0,2},{2,4},{4,6},{6,0},{1,3},{3,5},{5,7},{7,1},{8,10},{10,12},{12... | collective-permute-start | bytes 294920 | tf_op jit(solution)/shard_map/ppermute | solution.py:353
  140.9 22.1 %collective-permute-start.32 = (bf16[4,24,2048]{2,1,0:T(8,128)(2,1)}, bf16[4,24,2048]{2,1,0:T(8,128)(2,1)S(1)}, u32[]{:S(2)}, u32[]{:S(2)}) collective-permute-start(bf16[4,24,2048]{2,1,0:T(8,128)(2,1)} %collective-permute-done.31), channel_id=1, source_target_pairs={{0,1},{1,0},{2,3},{3,2},{4,5},{5,4},{6,7},{7,6},{8,9},{9,8},{10,11... | collective-permute-start | bytes 1179656 | tf_op jit(solution)/shard_map/ppermute | solution.py:347
  141.5 22.5 %collective-permute-start.30 = (bf16[4,24,2048]{2,1,0:T(8,128)(2,1)S(1)}, bf16[4,24,2048]{2,1,0:T(8,128)(2,1)S(1)}, u32[]{:S(2)}, u32[]{:S(2)}) collective-permute-start(bf16[4,24,2048]{2,1,0:T(8,128)(2,1)S(1)} %constant_dynamic-slice_fusion), channel_id=1, source_target_pairs={{0,1},{1,0},{2,3},{3,2},{4,5},{5,4},{6,7},{7,6},{8,9},{9,8},{10,11... | collective-permute-start | bytes 1179656 | tf_op jit(solution)/shard_map/ppermute | solution.py:347
  142.9 18.0 %collective-permute-start.28 = (bf16[4,24,4864]{2,1,0:T(8,128)(2,1)}, bf16[4,24,4864]{2,1,0:T(8,128)(2,1)S(1)}, u32[]{:S(2)}, u32[]{:S(2)}) collective-permute-start(bf16[4,24,4864]{2,1,0:T(8,128)(2,1)} %collective-permute-done.26), channel_id=1, source_target_pairs={{0,16},{8,24},{16,0},{24,8},{1,17},{9,25},{17,1},{25,9},{2,18},{10... | collective-permute-start | bytes 2801672 | tf_op jit(solution)/shard_map/ppermute | solution.py:344
  203.1 136.4 %collective-permute-start.64 = (bf16[384,4096]{1,0:T(8,128)(2,1)}, bf16[384,4096]{1,0:T(8,128)(2,1)}, u32[]{:S(2)}, u32[]{:S(2)}) collective-permute-start(bf16[384,4096]{1,0:T(8,128)(2,1)} %convolution_convert_fusion), channel_id=1, source_target_pairs={{0,8},{8,0},{16,24},{24,16},{1,9},{9,1},{17,25},{25,17},{2,10},{10... | collective-permute-start | bytes 9437192 | tf_op jit(solution)/shard_map/ppermute | solution.py:341
  204.3 50.9 %collective-permute-start.61 = (bf16[384,768]{1,0:T(8,128)(2,1)}, bf16[384,768]{1,0:T(8,128)(2,1)}, u32[]{:S(2)}, u32[]{:S(2)}) collective-permute-start(bf16[384,768]{1,0:T(8,128)(2,1)} %convolution_convert_fusion.3), channel_id=1, source_target_pairs={{0,8},{8,0},{16,24},{24,16},{1,9},{9,1},{17,25},{25,17},{2,10},{10... | collective-permute-start | bytes 1769480 | tf_op jit(solution)/shard_map/ppermute | solution.py:341
  206.6 87.4 %collective-permute-start.58 = (bf16[384,2048]{1,0:T(8,128)(2,1)}, bf16[384,2048]{1,0:T(8,128)(2,1)}, u32[]{:S(2)}, u32[]{:S(2)}) collective-permute-start(bf16[384,2048]{1,0:T(8,128)(2,1)} %convolution_convert_fusion.1), channel_id=1, source_target_pairs={{0,8},{8,0},{16,24},{24,16},{1,9},{9,1},{17,25},{25,17},{2,10},{10... | collective-permute-start | bytes 4718600 | tf_op jit(solution)/shard_map/ppermute | solution.py:341
  224.1 22.8 %collective-permute-start.40 = (bf16[384,256]{1,0:T(8,128)(2,1)}, bf16[384,256]{1,0:T(8,128)(2,1)S(1)}, u32[]{:S(2)}, u32[]{:S(2)}) collective-permute-start(bf16[384,256]{1,0:T(8,128)(2,1)} %get-tuple-element.88), channel_id=1, source_target_pairs={{0,1},{1,0},{2,3},{3,2},{4,5},{5,4},{6,7},{7,6},{8,9},{9,8},{10,11... | collective-permute-start | bytes 589832 | tf_op jit(solution)/shard_map/ppermute | solution.py:370
  255.3 15.9 %collective-permute-start.45 = (bf16[384,256]{1,0:T(8,128)(2,1)S(1)}, bf16[384,256]{1,0:T(8,128)(2,1)S(1)}, u32[]{:S(2)}, u32[]{:S(2)}) collective-permute-start(bf16[384,256]{1,0:T(8,128)(2,1)S(1)} %add_convert_fusion.7), channel_id=1, source_target_pairs={{0,4},{2,6},{4,0},{6,2},{1,5},{3,7},{5,1},{7,3},{8,12},{10,14},{12... | collective-permute-start | bytes 589832 | tf_op jit(solution)/shard_map/ppermute | solution.py:353
  261.6 18.8 %collective-permute-start.62 = (bf16[4,2,24,768]{3,2,0,1:T(8,128)(2,1)S(1)}, bf16[4,2,24,768]{3,2,0,1:T(8,128)(2,1)S(1)}, u32[]{:S(2)}, u32[]{:S(2)}) collective-permute-start(bf16[4,2,24,768]{3,2,0,1:T(8,128)(2,1)S(1)} %bitcast.388), channel_id=1, source_target_pairs={{0,16},{8,24},{16,0},{24,8},{1,17},{9,25},{17,1},{25,9},{2,18},{10... | collective-permute-start | bytes 884744 | tf_op jit(solution)/shard_map/ppermute | solution.py:344
  276.1 19.9 %collective-permute-start.50 = (bf16[384,1536]{1,0:T(8,128)(2,1)S(1)}, bf16[384,1536]{1,0:T(8,128)(2,1)S(1)}, u32[]{:S(2)}, u32[]{:S(2)}) collective-permute-start(bf16[384,1536]{1,0:T(8,128)(2,1)S(1)} %convolution_convert_fusion.2), channel_id=1, source_target_pairs={{0,8},{8,0},{16,24},{24,16},{1,9},{9,1},{17,25},{25,17},{2,10},{10... | collective-permute-start | bytes 3538952 | tf_op jit(solution)/shard_map/ppermute | solution.py:341
  298.5 24.6 %collective-permute-start.59 = (bf16[2,4,24,2048]{3,2,1,0:T(8,128)(2,1)S(1)}, bf16[2,4,24,2048]{3,2,1,0:T(8,128)(2,1)S(1)}, u32[]{:S(2)}, u32[]{:S(2)}) collective-permute-start(bf16[2,4,24,2048]{3,2,1,0:T(8,128)(2,1)S(1)} %dynamic-slice_bitcast_fusion.1), channel_id=1, source_target_pairs={{0,1},{1,0},{2,3},{3,2},{4,5},{5,4},{6,7},{7,6},{8,9},{9,8},{10,11... | collective-permute-start | bytes 2359304 | tf_op jit(solution)/shard_map/ppermute | solution.py:347
  306.7 16.7 %collective-permute-start.54 = (bf16[4,24,768]{2,1,0:T(8,128)(2,1)S(1)}, bf16[4,24,768]{2,1,0:T(8,128)(2,1)S(1)}, u32[]{:S(2)}, u32[]{:S(2)}) collective-permute-start(bf16[4,24,768]{2,1,0:T(8,128)(2,1)S(1)} %dynamic-slice_bitcast_fusion.14), channel_id=1, source_target_pairs={{0,16},{8,24},{16,0},{24,8},{1,17},{9,25},{17,1},{25,9},{2,18},{10... | collective-permute-start | bytes 442376 | tf_op jit(solution)/shard_map/ppermute | solution.py:344
  308.3 16.4 %collective-permute-start.52 = (bf16[4,24,768]{2,1,0:T(8,128)(2,1)S(1)}, bf16[4,24,768]{2,1,0:T(8,128)(2,1)S(1)}, u32[]{:S(2)}, u32[]{:S(2)}) collective-permute-start(bf16[4,24,768]{2,1,0:T(8,128)(2,1)S(1)} %dynamic-slice_bitcast_fusion.15), channel_id=1, source_target_pairs={{0,1},{1,0},{2,3},{3,2},{4,5},{5,4},{6,7},{7,6},{8,9},{9,8},{10,11... | collective-permute-start | bytes 442376 | tf_op jit(solution)/shard_map/ppermute | solution.py:347
  331.1 16.3 %collective-permute-start.60 = (bf16[4,24,2048]{2,1,0:T(8,128)(2,1)}, bf16[4,24,2048]{2,1,0:T(8,128)(2,1)}, u32[]{:S(2)}, u32[]{:S(2)}) collective-permute-start(bf16[4,24,2048]{2,1,0:T(8,128)(2,1)} %dynamic-slice_bitcast_fusion.4), channel_id=1, source_target_pairs={{0,16},{8,24},{16,0},{24,8},{1,17},{9,25},{17,1},{25,9},{2,18},{10... | collective-permute-start | bytes 1179656 | tf_op jit(solution)/shard_map/ppermute | solution.py:344
  343.6 15.7 %collective-permute-start.67 = (bf16[2,4,24,2048]{3,2,1,0:T(8,128)(2,1)}, bf16[2,4,24,2048]{3,2,1,0:T(8,128)(2,1)}, u32[]{:S(2)}, u32[]{:S(2)}) collective-permute-start(bf16[2,4,24,2048]{3,2,1,0:T(8,128)(2,1)} %dynamic-slice_bitcast_fusion), channel_id=1, source_target_pairs={{0,1},{1,0},{2,3},{3,2},{4,5},{5,4},{6,7},{7,6},{8,9},{9,8},{10,11... | collective-permute-start | bytes 2359304 | tf_op jit(solution)/shard_map/ppermute | solution.py:347
  347.6 19.3 %collective-permute-start.65 = (bf16[4,2,24,2048]{3,2,0,1:T(8,128)(2,1)S(1)}, bf16[4,2,24,2048]{3,2,0,1:T(8,128)(2,1)S(1)}, u32[]{:S(2)}, u32[]{:S(2)}) collective-permute-start(bf16[4,2,24,2048]{3,2,0,1:T(8,128)(2,1)S(1)} %bitcast.382), channel_id=1, source_target_pairs={{0,16},{8,24},{16,0},{24,8},{1,17},{9,25},{17,1},{25,9},{2,18},{10... | collective-permute-start | bytes 2359304 | tf_op jit(solution)/shard_map/ppermute | solution.py:344
  376.4 28.3 %collective-permute-start.70 = (bf16[24,6912]{1,0:T(8,128)(2,1)S(1)}, bf16[24,6912]{1,0:T(8,128)(2,1)S(1)}, u32[]{:S(2)}, u32[]{:S(2)}) collective-permute-start(bf16[24,6912]{1,0:T(8,128)(2,1)S(1)} %get-tuple-element.140), channel_id=1, source_target_pairs={{0,4},{2,6},{4,0},{6,2},{1,5},{3,7},{5,1},{7,3},{8,12},{10,14},{12... | collective-permute-start | bytes 995336 | tf_op jit(solution)/shard_map/ppermute | solution.py:350
  378.3 26.5 %collective-permute-start.69 = (bf16[24,6912]{1,0:T(8,128)(2,1)S(1)}, bf16[24,6912]{1,0:T(8,128)(2,1)S(1)}, u32[]{:S(2)}, u32[]{:S(2)}) collective-permute-start(bf16[24,6912]{1,0:T(8,128)(2,1)S(1)} %get-tuple-element.138), channel_id=1, source_target_pairs={{0,2},{2,4},{4,6},{6,0},{1,3},{3,5},{5,7},{7,1},{8,10},{10,12},{12... | collective-permute-start | bytes 995336 | tf_op jit(solution)/shard_map/ppermute | solution.py:350
  (99 other events, 884.5 us)
where the time goes:
time: 415 us; the launch traced here: 407 us
  waiting for transfers between devices  203 us (49%)
  starting transfers between devices  86.7 us (21%)
  local copies, waits for them, and re-layouts  39.6 us (10%)
  Pallas kernels  30.2 us (7%)
  matrix products  26.1 us (6%)
  other arithmetic  18.1 us (4%)
    ppermute x12, waiting for transfers between devices, over_blk(): lax.ppermute(value, 'blk', [(i, (i + shift) % blk_size) for i in range(bl...  57.5 us
    ppermute x13, waiting for transfers between devices, over_y(): return lax.ppermute(value, 'ulysses', [(i, i ^ 1) for i in range(uly_size)])  47.6 us
    ppermute x18, waiting for transfers between devices, over_part(): lax.ppermute(value, 'blk', [(i, i - i % head_parts + (i + shift) % head_p...  37.1 us
    ppermute x13, waiting for transfers between devices, over_x(): return lax.ppermute(value, 'dp', [(i, i ^ 2) for i in range(dp_size)])  33.1 us
    dot_general x19, matrix products, dot(): lax.dot_general(left, right, (((left_dim,), (right_dim,)), ((), ())), pre...  26.1 us
    ppermute x13, starting transfers between devices, over_x(): return lax.ppermute(value, 'dp', [(i, i ^ 2) for i in range(dp_size)])  22.9 us
    ppermute x8, waiting for transfers between devices, over_member(): return lax.ppermute(value, ('blk', 'ulysses'), pairs)  22 us
    ppermute x12, starting transfers between devices, over_blk(): lax.ppermute(value, 'blk', [(i, (i + shift) % blk_size) for i in range(bl...  20.9 us
  transfers between devices with their start and end apart: 72, of which 37 were waited for; matrix products, arithmetic and copies ran while one was open for 13% of the time, Pallas kernels for 7%

commit v1 on v0

--- a/solution.py
+++ b/solution.py
@@ -301,6 +301,179 @@
     return outs[:count], outs[count:]
 
 
+def feed_forward_kernel(hidden_units, parts, place_ref, length_ref, *refs):
+    attn_pieces, refs = refs[:parts], refs[parts:]
+    (tokens_ref, cotangent_ref, gain_ref), refs = refs[:3], refs[3:]
+    others, downs, refs = refs[:4], refs[4:8], refs[8:]
+    douts, refs = refs[:parts], refs[parts:]
+    (output_ref, d_middle_ref, attn_far_ref, attn_near_ref, d_branch_ref), refs = refs[:5], refs[5:]
+    grad_outs, refs = refs[:4], refs[4:]
+    out_s, gate_up_s, down_s, d_normed_s, turned_s, middle_s, d_attn_s = refs[:7]
+    rows_s, grads_s, sems, grad_sems = refs[7:11], refs[11:15], refs[15], refs[16]
+    rows, width = tokens_ref.shape
+    core, part, stretch, x_at = place_ref[0], place_ref[1], place_ref[2], place_ref[3]
+    quarter = width // 4
+    copies = []
+    for index, (columns, target, sources) in enumerate(
+        (
+            (slice(0, width), out_s, others),
+            (slice(width, width + 2 * hidden_units), gate_up_s, others),
+            (slice(0, hidden_units), down_s, downs),
+        )
+    ):
+        group = []
+        for which, source in enumerate(sources):
+            x, c = (x_at + which // 2) % 2, (core + which) % 2
+            start = pl.multiple_of((2 * x + c) * quarter, 64)
+            group.append(
+                pltpu.make_async_copy(
+                    source.at[:, columns],
+                    target.at[pl.ds(start, quarter), :],
+                    sems.at[index, which],
+                )
+            )
+        copies.append(group)
+    for group in copies:
+        for copy in group:
+            copy.start()
+
+    def by_core(source, far, near):
+        for x in range(2):
+            for ref, index in ((far, 1 - core), (near, core)):
+                start = pl.multiple_of((2 * x + index) * quarter, 64)
+                ref[x * quarter : (x + 1) * quarter, :] = source[pl.ds(start, quarter), :]
+
+    part_width = width // parts
+    for shift, piece in enumerate(attn_pieces):
+        start = pl.multiple_of((part + shift) % parts * part_width, 64)
+        d_attn_s[pl.ds(start, part_width), :] = piece[...]
+    by_core(d_attn_s, attn_far_ref, attn_near_ref)
+    position = stretch * rows + lax.broadcasted_iota(jnp.int32, (rows, width), 0)
+    d_out = jnp.where(position < length_ref[0], cotangent_ref[...].astype(F32), 0.0)
+    d_down = (BRANCH_SCALE * d_out).astype(BF16)
+    turned_s[...] = jnp.transpose(d_down)
+    by_core(turned_s, rows_s[0], rows_s[1])
+    attn = jnp.transpose(d_attn_s[...])
+    gain = gain_ref[...]
+    for copy in copies[0]:
+        copy.wait()
+    middle = tokens_ref[...].astype(F32) + BRANCH_SCALE * jnp.dot(
+        attn, out_s[...], preferred_element_type=F32
+    )
+    middle_s[...] = middle
+    inverse = lax.rsqrt(jnp.mean(middle * middle, axis=-1, keepdims=True) + NORM_EPS)
+    normed = (middle * inverse * gain).astype(BF16)
+    turned_s[...] = jnp.transpose(normed)
+    by_core(turned_s, rows_s[2], rows_s[3])
+    d_normed_s[...] = jnp.zeros_like(d_normed_s)
+    output_ref[...] = middle
+    for copy in copies[1] + copies[2]:
+        copy.wait()
+    step = 256
+    steps = hidden_units // step
+
+    def leaving(index):
+        at = pl.ds(pl.multiple_of(index * step, step), step)
+        up_at = pl.ds(pl.multiple_of(hidden_units + index * step, step), step)
+        for which in range(2):
+            for columns in (at,):
+                yield pltpu.make_async_copy(
+                    grads_s[which].at[:, columns],
+                    grad_outs[which].at[:, columns],
+                    grad_sems.at[which, index],
+                )
+            for name, columns in enumerate((at, up_at)):
+                yield pltpu.make_async_copy(
+                    grads_s[2 + which].at[:, columns],
+                    grad_outs[2 + which].at[:, columns],
+                    grad_sems.at[2 + 2 * which + name, index],
+                )
+
+    def chunk(index, carry):
+        at = pl.ds(pl.multiple_of(index * step, step), step)
+        up_at = pl.ds(pl.multiple_of(hidden_units + index * step, step), step)
+        w_gate, w_up = gate_up_s[:, at], gate_up_s[:, up_at]
+        gate = jnp.dot(normed, w_gate, preferred_element_type=F32)
+        up = jnp.dot(normed, w_up, preferred_element_type=F32)
+        d_hidden = jnp.dot(d_down, down_s[:, at], preferred_element_type=F32)
+        sigma = jax.nn.sigmoid(gate)
+        silu = gate * sigma
+        hidden = (silu * up).astype(BF16)
+        d_gate = (d_hidden * up * sigma * (1.0 + gate * (1.0 - sigma))).astype(BF16)
+        d_up = (d_hidden * silu).astype(BF16)
+        output_ref[...] += BRANCH_SCALE * dot(hidden, down_s[:, at], 1, 1)
+        d_normed_s[...] += dot(d_gate, w_gate, 1, 1) + dot(d_up, w_up, 1, 1)
+        for which in range(2):
+            grads_s[which][:, at] = dot(rows_s[which][...], hidden, 1, 0).astype(BF16)
+            grads_s[2 + which][:, at] = dot(rows_s[2 + which][...], d_gate, 1, 0).astype(BF16)
+            grads_s[2 + which][:, up_at] = dot(rows_s[2 + which][...], d_up, 1, 0).astype(BF16)
+        for copy in leaving(index):
+            copy.start()
+        return carry
+
+    lax.fori_loop(0, steps, chunk, 0)
+    middle = middle_s[...]
+    scaled = middle * inverse
+    d_scaled = d_normed_s[...] * gain
+    d_middle = d_out + norm_back(d_scaled, scaled, inverse)
+    d_middle_ref[...] = d_middle
+    d_branch = (BRANCH_SCALE * d_middle).astype(BF16)
+    d_branch_ref[...] = d_branch
+    d_attn_s[...] = dot(out_s[...], d_branch, 1, 1).astype(BF16)
+    for shift, dout in enumerate(douts):
+        start = pl.multiple_of((part + shift) % parts * part_width, 64)
+        dout[...] = d_attn_s[pl.ds(start, part_width), :]
+
+    def left(index, carry):
+        for copy in leaving(index):
+            copy.wait()
+        return carry
+
+    lax.fori_loop(0, steps, left, 0)
+
+
+def feed_forward(parts, place, length, attn_pieces, tokens, cotangent, gain, others, downs):
+    rows, width = tokens.shape
+    hidden_units = downs[0].shape[-1]
+    shape = jax.ShapeDtypeStruct
+    half = shape((width // 2, rows), BF16)
+    grads = [(width // 2, hidden_units)] * 2 + [(width // 2, 2 * hidden_units)] * 2
+    quarters = (*others, *downs)
+    outs = pl.pallas_call(
+        functools.partial(feed_forward_kernel, hidden_units, parts),
+        out_shape=(shape((width // parts, rows), BF16),) * parts
+        + (
+            shape((rows, width), F32),
+            shape((rows, width), F32),
+            half,
+            half,
+            shape((rows, width), BF16),
+        )
+        + tuple(shape(grad, BF16) for grad in grads),
+        in_specs=[in_smem()] * 2
+        + [in_vmem()] * (parts + 3)
+        + [pl.BlockSpec(memory_space=pl.ANY)] * 8,
+        out_specs=(in_vmem(),) * (parts + 5) + (pl.BlockSpec(memory_space=pl.ANY),) * 4,
+        scratch_shapes=[
+            pltpu.VMEM((width, width), BF16),
+            pltpu.VMEM((width, 2 * hidden_units), BF16),
+            pltpu.VMEM((width, hidden_units), BF16),
+            pltpu.VMEM((rows, width), F32),
+            pltpu.VMEM((width, rows), BF16),
+            pltpu.VMEM((rows, width), F32),
+            pltpu.VMEM((width, rows), BF16),
+        ]
+        + [pltpu.VMEM((width // 2, rows), BF16)] * 4
+        + [pltpu.VMEM(grad, BF16) for grad in grads]
+        + [
+            pltpu.SemaphoreType.DMA((3, 4)),
+            pltpu.SemaphoreType.DMA((6, hidden_units // 256)),
+        ],
+        name="feed_forward",
+    )(place, length, *attn_pieces, tokens, cotangent, gain.reshape(1, width), *quarters)
+    return outs[:parts], outs[parts : parts + 5], outs[parts + 5 :]
+
+
 def local(
     tokens,
     cotangent,
@@ -381,7 +554,6 @@
     stretches = jnp.sum(
         jnp.where(places[:, None] == labels[None, :], stretch_order[None, :], 0), axis=1
     ).astype(jnp.int32)
-    length = lengths[0]
 
     own_pos = stretches[0] * rows + jnp.arange(rows, dtype=jnp.int32)
     half_dim = HEAD_DIM // 2
@@ -407,10 +579,11 @@
         second_xy = over_x(second_y)
         first_y = over_y(first)
         first_xy = over_y(first_x)
-        return (
-            plane(first, first_x, first_y, first_xy),
-            plane(second, second_x, second_y, second_xy),
-        )
+        return (first, first_x, first_y, first_xy), (second, second_x, second_y, second_xy)
+
+    def column_pair(mine, by_y):
+        here = lax.broadcasted_iota(jnp.int32, (1, 2, 1, 1), 1) == uly_at
+        return jnp.where(here, mine[:, None], by_y[:, None]).reshape(width // 4, -1)
 
     def plane(mine, by_x, by_y, by_xy):
         return in_order(
@@ -445,7 +618,7 @@
     )
     qkv_firsts = plane_first(*qkv_halves)
     qkv_planes = plane_second(*qkv_halves, *qkv_firsts)
-    qkv_half = jnp.concatenate(qkv_planes, axis=-1)
+    qkv_half = jnp.concatenate([plane(*pieces) for pieces in qkv_planes], axis=-1)
     qkv_all = both_cores(lax.optimization_barrier(qkv_half))
     gain_attn_all = qkv_all[:, 0].astype(F32)
     gain_ffn_all = qkv_all[:, 1].astype(F32)
@@ -463,9 +636,6 @@
             pick(grid, core, 1).reshape(width // 2, rows) for core in (1 - core_at, core_at)
         )
 
-    live = (own_pos < length).astype(F32)
-    d_out = cotangent.astype(F32) * live[:, None]
-    d_down = (BRANCH_SCALE * d_out).astype(BF16)
     inputs = tokens.astype(F32)
     scaled_in, inverse_in = normalize(inputs)
     normed_attn = (scaled_in * gain_attn_all[None, :]).astype(BF16)
@@ -486,12 +656,15 @@
             result.append(over_part(piece, shift) if shift else piece)
         return result
 
-    def return_parts(pieces, *earlier):
-        back = [
+    def send_back(pieces, *earlier):
+        return [
             after(over_part(piece, head_parts - shift), *earlier) if shift else piece
             for shift, piece in enumerate(pieces)
         ]
-        return roll_to(jnp.stack(back), (head_parts - part_at) % head_parts)
+
+    def return_parts(pieces, *earlier):
+        back = jnp.stack(send_back(pieces, *earlier))
+        return roll_to(back, (head_parts - part_at) % head_parts)
 
     keys = scatter_parts(kv_send.reshape(head_parts, 2 * part_width, rows))
     queries = scatter_parts(q_send.reshape(head_parts, part_width, rows))
@@ -507,60 +680,70 @@
         (rest_line[..., :hidden_units], rest_line[..., hidden_units:])
     )
     rest_firsts = plane_first(*rest_halves)
+    other_mine = rest_halves[1][:, None]
+    other_mine = jnp.broadcast_to(other_mine, (blk_size, 2) + other_mine.shape[2:])
+    other_mine = lax.dynamic_update_slice(
+        other_mine, rest_firsts[1][:, None], (0, 1 - uly_at, 0, 0)
+    )
+    other_mine = lax.optimization_barrier(other_mine.reshape(width // 4, -1))
+    other_mine_core = over_core(other_mine)
     rest_planes = plane_second(
         *(after(piece, keys[-1]) for piece in rest_halves),
         *(after(piece, keys[-1]) for piece in rest_firsts),
     )
-    down_half, other_half = rest_planes
-
-    d_down_rows, normed_rows, lengths = lax.optimization_barrier(
-        (by_core(jnp.transpose(d_down)), by_core(jnp.transpose(normed_attn)), lengths)
+    (first, first_x, first_y, first_xy), (_, second_x, _, second_xy) = rest_planes
+    other_x = lax.optimization_barrier(column_pair(second_x, second_xy))
+    down_mine = lax.optimization_barrier(column_pair(first, first_y))
+    down_x = lax.optimization_barrier(column_pair(first_x, first_xy))
+    others = (other_mine, other_mine_core, other_x, over_core(other_x))
+    downs = (down_mine, over_core(down_mine), down_x, over_core(down_x))
+    normed_rows, lengths = lax.optimization_barrier(
+        (by_core(jnp.transpose(normed_attn)), lengths)
     )
     outs, exact_t, logsum = attention_forward(stretches, lengths, queries, keys, group)
-    down_all = both_cores(lax.optimization_barrier(down_half))
-    other_all = both_cores(lax.optimization_barrier(other_half))
-    out_all = other_all[:, :width]
-    gate_up_all = other_all[:, width:]
-
-    attn_t = return_parts(outs).reshape(width, rows)
-
-    middle = inputs + BRANCH_SCALE * dot(attn_t, out_all, 0, 0)
-    scaled_mid, inverse_mid = normalize(middle)
-    normed_ffn = (scaled_mid * gain_ffn_all[None, :]).astype(BF16)
-    gate_up = dot(normed_ffn, gate_up_all, 1, 0)
-    gate_act = gate_up[:, :hidden_units]
-    upward = gate_up[:, hidden_units:]
-    sigma = jax.nn.sigmoid(gate_act)
-    silu_act = gate_act * sigma
-    hidden = (silu_act * upward).astype(BF16)
-    output = middle + BRANCH_SCALE * dot(hidden, down_all, 1, 1)
-
-    d_hidden = dot(d_down, down_all, 1, 0)
-    d_gate = (d_hidden * upward * sigma * (1.0 + gate_act * (1.0 - sigma))).astype(BF16)
-    d_up = (d_hidden * silu_act).astype(BF16)
-    d_gate_up = jnp.concatenate([d_gate, d_up], axis=1)
-    d_normed_ffn = dot(d_gate_up, gate_up_all, 1, 1)
-    d_middle = d_out + norm_back(d_normed_ffn * gain_ffn_all[None, :], scaled_mid, inverse_mid)
-    d_branch = (BRANCH_SCALE * d_middle).astype(BF16)
-    d_attn_t = dot(out_all, d_branch, 1, 1).astype(BF16)
-    douts = scatter_parts(d_attn_t.reshape(head_parts, part_width, rows))
+    attn_pieces = send_back(outs)
+
+    d_attns, (output, d_middle, *attn_rows, d_branch), rest_grads = feed_forward(
+        head_parts,
+        jnp.stack([core_at, part_at, stretches[0], x_at]).astype(jnp.int32),
+        lengths,
+        attn_pieces,
+        tokens,
+        cotangent,
+        gain_ffn_all,
+        others,
+        downs,
+    )
+
+    douts = [
+        over_part(piece, shift) if shift else piece for shift, piece in enumerate(d_attns)
+    ]
 
     def both(mine, theirs):
         return (mine.astype(F32) + theirs.astype(F32)).astype(BF16)
 
     def core_sum(left_rows, product):
         far = product(left_rows[0]).astype(BF16)
-        near = product(left_rows[1])
+        return core_pair(far, product(left_rows[1]))
+
+    def core_pair(far, near):
         arrived = over_core(far)
-        return both(near, arrived).reshape(2, blk_size, 2, shard, -1)
-
-    def x_sum(values, *earlier):
-        arrived = over_x(pick(values, 1 - x_at, 0))
-        return both(pick(values, x_at, 0), after(arrived, *earlier))
-
-    def y_sum(values, axis, *earlier):
-        arrived = over_y(pick(values, 1 - uly_at, axis))
-        return both(pick(values, uly_at, axis), after(arrived, *earlier))
+        shape = (2, blk_size, 2, shard, -1)
+        return near.reshape(shape), arrived.reshape(shape)
+
+    def columns(terms, span):
+        return tuple(term[..., span] for term in terms)
+
+    def added(terms, index, axis):
+        return sum(pick(term, index, axis).astype(F32) for term in terms).astype(BF16)
+
+    def x_sum(terms, *earlier):
+        arrived = over_x(added(terms, 1 - x_at, 0))
+        return both(added(terms, x_at, 0), after(arrived, *earlier))
+
+    def y_sum(terms, axis, *earlier):
+        arrived = over_y(added(terms, 1 - uly_at, axis))
+        return both(added(terms, uly_at, axis), after(arrived, *earlier))
 
     def line_sum(values, *earlier):
         total = pick(values, blk_at, 0).astype(F32)
@@ -569,9 +752,9 @@
             total = total + after(over_blk(piece, shift), *earlier).astype(F32)
         return total
 
-    down_core = core_sum(d_down_rows, lambda l: dot(l, hidden, 1, 0))
-    gate_up_core = core_sum(by_core(jnp.transpose(normed_ffn)), lambda l: dot(l, d_gate_up, 1, 0))
-    out_core = core_sum(by_core(attn_t), lambda l: dot(l, d_branch, 1, 0))
+    down_sum_core = core_pair(rest_grads[0], rest_grads[1])
+    gate_up_core = core_pair(rest_grads[2], rest_grads[3])
+    out_core = core_sum(attn_rows, lambda l: dot(l, d_branch, 1, 0))
 
     dq, dkv = attention_backward(stretches, lengths, queries, keys, douts, exact_t, logsum, group)
     d_q = return_parts(dq).reshape(HEADS, HEAD_DIM, rows)
@@ -584,25 +767,26 @@
             theirs = dkv[member_shift * head_parts + shift]
             total = total + over_member(theirs, members - member_shift).astype(F32)
         back.append(total.astype(BF16))
-    d_kv = return_parts(back, q_core)
+    d_kv = return_parts(back, *q_core)
     q_x = x_sum(q_core)
-    gate_x = x_sum(gate_up_core[..., :hidden_units], back[-1])
-    up_y = y_sum(gate_up_core[..., hidden_units:], 2, dkv[0])
-    gate_sum = y_sum(gate_x, 1, d_kv)
-    up_sum = x_sum(up_y, back[-1])
-    down_sum = x_sum(y_sum(down_core, 2, dkv[0]), back[-1])
-    out_sum = y_sum(x_sum(out_core, back[-1]), 1, d_kv)
+    gate_x = x_sum(columns(gate_up_core, slice(0, hidden_units)), back[-1])
+    up_y = y_sum(columns(gate_up_core, slice(hidden_units, None)), 2, dkv[0])
+    gate_sum = y_sum((gate_x,), 1, d_kv)
+    up_sum = x_sum((up_y,), back[-1])
+    down_y = y_sum(down_sum_core, 2, dkv[0])
+    down_sum = x_sum((down_y,), back[-1])
+    out_sum = y_sum((x_sum(out_core, back[-1]),), 1, d_kv)
     d_kv = d_kv.reshape(head_parts, 2, group, HEAD_DIM, rows)
     d_kv_t = jnp.stack(
         [rotate(d_kv[:, 0].astype(F32), -1.0).astype(BF16), d_kv[:, 1]], axis=1
     ).reshape(2 * width, rows)
 
     kv_core = core_sum(normed_rows, lambda l: dot(l, d_kv_t, 1, 1))
-    k_x = x_sum(kv_core[..., :width])
-    v_y = y_sum(kv_core[..., width:], 2)
-    q_sum = y_sum(q_x, 1)
-    k_sum = y_sum(k_x, 1)
-    v_sum = x_sum(v_y)
+    k_x = x_sum(columns(kv_core, slice(0, width)))
+    v_y = y_sum(columns(kv_core, slice(width, None)), 2)
+    q_sum = y_sum((q_x,), 1)
+    k_sum = y_sum((k_x,), 1)
+    v_sum = x_sum((v_y,))
 
     rest_sum = line_sum(jnp.concatenate([down_sum, out_sum, gate_sum, up_sum], axis=-1), q_sum, k_sum, v_sum)
     qkv_sum = line_sum(jnp.concatenate([q_sum, k_sum, v_sum], axis=-1))

time: 415 us -> 426 us (1.027); the launches traced: 407 us -> 425 us
  waiting for transfers between devices: 203 us -> 239 us
  matrix products: 26.1 us -> 5.85 us
  Pallas kernels: 30.2 us -> 49.4 us
  starting transfers between devices: 86.7 us -> 73.2 us
    ppermute x18, waiting for transfers between devices: 37.1 us -> 57.9 us  [over_part(): lax.ppermute(value, 'blk', [(i, i - i % head_parts + (i + shift) % head_p...]
    dot_general x19 -> x9, matrix products: 26.1 us -> 5.85 us  [dot(): lax.dot_general(left, right, (((left_dim,), (right_dim,)), ((), ())), pre...]
    pallas_call x0 -> x1, Pallas kernels: none -> 19.1 us  [feed_forward(): pl.pallas_call(functools.partial(feed_forward_kernel, hidden_units, parts...]
    ppermute x13, waiting for transfers between devices: 33.1 us -> 44 us  [over_x(): return lax.ppermute(value, 'dp', [(i, i ^ 2) for i in range(dp_size)])]
    ppermute x13, waiting for transfers between devices: 47.6 us -> 56 us  [over_y(): return lax.ppermute(value, 'ulysses', [(i, i ^ 1) for i in range(uly_size)])]
    ppermute x8 -> x10, waiting for transfers between devices: 5.63 us -> 0.03 us  [over_core(): return lax.ppermute(value, 'dp', [(i, i ^ 1) for i in range(dp_size)])]
    ppermute x13, starting transfers between devices: 15.1 us -> 9.81 us  [over_y(): return lax.ppermute(value, 'ulysses', [(i, i ^ 1) for i in range(uly_size)])]
    ppermute x8, waiting for transfers between devices: 22 us -> 27.1 us  [over_member(): return lax.ppermute(value, ('blk', 'ulysses'), pairs)]
  transfers between devices with their start and end apart: 72 -> 74, of which waited for: 37 -> 42; matrix products, arithmetic and copies ran while one was open for 13% -> 10% of each run, Pallas kernels for 7% -> 7%
where the time goes in v1:
time: 426 us; the launch traced here: 425 us
  waiting for transfers between devices  239 us (56%)
  starting transfers between devices  73.2 us (17%)
  Pallas kernels  49.4 us (12%)
  local copies, waits for them, and re-layouts  35.5 us (8%)
  other arithmetic  18.4 us (4%)
  matrix products  5.85 us (1%)
    ppermute x18, waiting for transfers between devices, over_part(): lax.ppermute(value, 'blk', [(i, i - i % head_parts + (i + shift) % head_p...  57.9 us
    ppermute x13, waiting for transfers between devices, over_y(): return lax.ppermute(value, 'ulysses', [(i, i ^ 1) for i in range(uly_size)])  56 us
    ppermute x12, waiting for transfers between devices, over_blk(): lax.ppermute(value, 'blk', [(i, (i + shift) % blk_size) for i in range(bl...  54.1 us
    ppermute x13, waiting for transfers between devices, over_x(): return lax.ppermute(value, 'dp', [(i, i ^ 2) for i in range(dp_size)])  44 us
    ppermute x8, waiting for transfers between devices, over_member(): return lax.ppermute(value, ('blk', 'ulysses'), pairs)  27.1 us
    ppermute x13, starting transfers between devices, over_x(): return lax.ppermute(value, 'dp', [(i, i ^ 2) for i in range(dp_size)])  20.1 us
    pallas_call x1, Pallas kernels, feed_forward(): pl.pallas_call(functools.partial(feed_forward_kernel, hidden_units, parts...  19.1 us
    ppermute x12, starting transfers between devices, over_blk(): lax.ppermute(value, 'blk', [(i, (i + shift) % blk_size) for i in range(bl...  17.6 us
  transfers between devices with their start and end apart: 74, of which 42 were waited for; matrix products, arithmetic and copies ran while one was open for 10% of the time, Pallas kernels for 7%

profile of v1, /device:TPU:0, one launch (start us, length us, event | category | flops | bytes accessed | tf_op | source)
XLA Modules:
  0.0 424.5 jit_solution(2413168932055144090)
XLA Ops:
  3.2 5.1 %collective-permute-start = (bf16[24,2432]{1,0:T(8,128)(2,1)S(1)}, bf16[24,2432]{1,0:T(8,128)(2,1)S(1)}, u32[]{:S(2)}, u32[]{:S(2)}) collective-permute-start(bf16[24,2432]{1,0:T(8,128)(2,1)S(1)} %concatenate.124), channel_id=1, source_target_pairs={{0,6},{2,0},{4,2},{6,4},{1,7},{3,1},{5,3},{7,5},{8,14},{10,8},{12,... | collective-permute-start | bytes 350216 | tf_op jit(solution)/shard_map/ppermute | solution.py:523
  11.9 6.5 %collective-permute-done.1 = bf16[24,2432]{1,0:T(8,128)(2,1)S(1)} collective-permute-done((bf16[24,2432]{1,0:T(8,128)(2,1)S(1)}, bf16[24,2432]{1,0:T(8,128)(2,1)S(1)}, u32[]{:S(2)}, u32[]{:S(2)}) %collective-permute-start.1) | collective-permute-done | bytes 116768 | tf_op jit(solution)/shard_map/ppermute | solution.py:523
  22.8 4.2 %collective-permute-done.6 = bf16[4,24,1152]{2,1,0:T(8,128)(2,1)S(1)} collective-permute-done((bf16[4,24,1152]{2,1,0:T(8,128)(2,1)S(1)}, bf16[4,24,1152]{2,1,0:T(8,128)(2,1)S(1)}, u32[]{:S(2)}, u32[]{:S(2)}) %collective-permute-start.6) | collective-permute-done | bytes 221216 | tf_op jit(solution)/shard_map/ppermute | solution.py:520
  28.6 5.2 %collective-permute-done.4 = bf16[4,24,1280]{2,1,0:T(8,128)(2,1)S(1)} collective-permute-done((bf16[4,24,1280]{2,1,0:T(8,128)(2,1)S(1)}, bf16[4,24,1280]{2,1,0:T(8,128)(2,1)S(1)}, u32[]{:S(2)}, u32[]{:S(2)}) %collective-permute-start.4) | collective-permute-done | bytes 245792 | tf_op jit(solution)/shard_map/ppermute | solution.py:517
  36.9 3.1 collective-permute-done.5
  55.2 19.0 %collective-permute-done.24 = bf16[24,6912]{1,0:T(8,128)(2,1)S(1)} collective-permute-done((bf16[24,6912]{1,0:T(8,128)(2,1)S(1)}, bf16[24,6912]{1,0:T(8,128)(2,1)S(1)}, u32[]{:S(2)}, u32[]{:S(2)}) %collective-permute-start.24) | collective-permute-done | bytes 331808 | tf_op jit(solution)/shard_map/ppermute | solution.py:523
  75.1 6.1 %collective-permute-done.15.refs_7_ = bf16[384,256]{1,0:T(8,128)(2,1)S(1)} collective-permute-done((bf16[384,256]{1,0:T(8,128)(2,1)S(1)}, bf16[384,256]{1,0:T(8,128)(2,1)S(1)}, u32[]{:S(2)}, u32[]{:S(2)}) %collective-permute-start.15) | collective-permute-done | bytes 196640 | tf_op jit(solution)/shard_map/ppermute | solution.py:526
  84.4 16.6 %collective-permute-done.19.refs_11_ = bf16[384,256]{1,0:T(8,128)(2,1)S(1)} collective-permute-done((bf16[384,256]{1,0:T(8,128)(2,1)S(1)}, bf16[384,256]{1,0:T(8,128)(2,1)S(1)}, u32[]{:S(2)}, u32[]{:S(2)}) %collective-permute-start.19) | collective-permute-done | bytes 196640 | tf_op jit(solution)/shard_map/ppermute | solution.py:543
  105.1 18.6 %collective-permute-done.29 = bf16[4,24,4864]{2,1,0:T(8,128)(2,1)S(1)} collective-permute-done((bf16[4,24,4864]{2,1,0:T(8,128)(2,1)S(1)}, bf16[4,24,4864]{2,1,0:T(8,128)(2,1)S(1)}, u32[]{:S(2)}, u32[]{:S(2)}) %collective-permute-start.29) | collective-permute-done | bytes 933920 | tf_op jit(solution)/shard_map/ppermute | solution.py:517
  127.8 7.8 %collective-permute-done.33 = bf16[4,24,2048]{2,1,0:T(8,128)(2,1)S(1)} collective-permute-done((bf16[4,24,2048]{2,1,0:T(8,128)(2,1)S(1)}, bf16[4,24,2048]{2,1,0:T(8,128)(2,1)S(1)}, u32[]{:S(2)}, u32[]{:S(2)}) %collective-permute-start.33) | collective-permute-done | bytes 393248 | tf_op jit(solution)/shard_map/ppermute | solution.py:517
  139.8 4.2 collective-permute-done.11.refs_2_
  146.3 6.8 %collective-permute-done.13.refs_5_ = bf16[384,256]{1,0:T(8,128)(2,1)S(1)} collective-permute-done((bf16[384,256]{1,0:T(8,128)(2,1)S(1)}, bf16[384,256]{1,0:T(8,128)(2,1)S(1)}, u32[]{:S(2)}, u32[]{:S(2)}) %collective-permute-start.13) | collective-permute-done | bytes 196640 | tf_op jit(solution)/shard_map/ppermute | solution.py:526
  157.9 4.3 %collective-permute-done.14.refs_6_ = bf16[384,256]{1,0:T(8,128)(2,1)} collective-permute-done((bf16[384,256]{1,0:T(8,128)(2,1)S(1)}, bf16[384,256]{1,0:T(8,128)(2,1)}, u32[]{:S(2)}, u32[]{:S(2)}) %collective-permute-start.14) | collective-permute-done | bytes 196640 | tf_op jit(solution)/shard_map/ppermute | solution.py:526
  165.1 6.1 %collective-permute-done.18.refs_10_ = bf16[384,256]{1,0:T(8,128)(2,1)S(1)} collective-permute-done((bf16[384,256]{1,0:T(8,128)(2,1)}, bf16[384,256]{1,0:T(8,128)(2,1)S(1)}, u32[]{:S(2)}, u32[]{:S(2)}) %collective-permute-start.18) | collective-permute-done | bytes 196640 | tf_op jit(solution)/shard_map/ppermute | solution.py:543
  171.8 13.4 %attention_forward.1 = (bf16[192,256]{1,0:T(8,128)(2,1)}, bf16[192,256]{1,0:T(8,128)(2,1)}, bf16[192,256]{1,0:T(8,128)(2,1)}, bf16[192,256]{1,0:T(8,128)(2,1)}, ...) custom-call(s32[8]{0:T(128)} %copy-done.51, s32[1]{0:T(128)S(6)} %copy.227.length_ref, ...), custom_call_target="tpu_custom_call" | custom-call | tf_op jit(solution)/shard_map/attention_forward/pallas_call | solution.py:255
  192.4 5.6 %collective-permute-done.21.refs_2_ = bf16[192,256]{1,0:T(8,128)(2,1)S(1)} collective-permute-done((bf16[192,256]{1,0:T(8,128)(2,1)}, bf16[192,256]{1,0:T(8,128)(2,1)S(1)}, u32[]{:S(2)}, u32[]{:S(2)}) %collective-permute-start.21) | collective-permute-done | bytes 98336 | tf_op jit(solution)/shard_map/ppermute | solution.py:526
  198.6 6.0 %collective-permute-done.22.refs_3_ = bf16[192,256]{1,0:T(8,128)(2,1)S(1)} collective-permute-done((bf16[192,256]{1,0:T(8,128)(2,1)}, bf16[192,256]{1,0:T(8,128)(2,1)S(1)}, u32[]{:S(2)}, u32[]{:S(2)}) %collective-permute-start.22) | collective-permute-done | bytes 98336 | tf_op jit(solution)/shard_map/ppermute | solution.py:526
  205.2 19.1 %feed_forward.1 = (bf16[192,256]{1,0:T(8,128)(2,1)}, bf16[192,256]{1,0:T(8,128)(2,1)}, bf16[192,256]{1,0:T(8,128)(2,1)}, bf16[192,256]{1,0:T(8,128)(2,1)}, f32[2...) custom-call(s32[4]{0:T(128)} %pad_add_fusion.place_ref, ...), custom_call_target="tpu_custom_call" | custom-call | tf_op jit(solution)/shard_map/feed_forward/pallas_call | solution.py:442
  234.3 17.0 %attention_backward.1 = (bf16[192,256]{1,0:T(8,128)(2,1)}, bf16[192,256]{1,0:T(8,128)(2,1)}, bf16[192,256]{1,0:T(8,128)(2,1)}, bf16[192,256]{1,0:T(8,128)(2,1)},...) custom-call(s32[8]{0:T(128)} %copy-done.51, ...), custom_call_target="tpu_custom_call" | custom-call | tf_op jit(solution)/shard_map/attention_backward/pallas_call | solution.py:282
  255.0 3.2 collective-permute-done.39
  260.2 4.8 %collective-permute-done.40 = bf16[192,256]{1,0:T(8,128)(2,1)S(1)} collective-permute-done((bf16[192,256]{1,0:T(8,128)(2,1)}, bf16[192,256]{1,0:T(8,128)(2,1)S(1)}, u32[]{:S(2)}, u32[]{:S(2)}) %collective-permute-start.40) | collective-permute-done | bytes 98336 | tf_op jit(solution)/shard_map/ppermute | solution.py:526
  265.0 6.6 %collective-permute-done.41 = bf16[192,256]{1,0:T(8,128)(2,1)S(1)} collective-permute-done((bf16[192,256]{1,0:T(8,128)(2,1)}, bf16[192,256]{1,0:T(8,128)(2,1)S(1)}, u32[]{:S(2)}, u32[]{:S(2)}) %collective-permute-start.41) | collective-permute-done | bytes 98336 | tf_op jit(solution)/shard_map/ppermute | solution.py:526
  287.5 6.2 %collective-permute-done.47 = bf16[384,256]{1,0:T(8,128)(2,1)S(1)} collective-permute-done((bf16[384,256]{1,0:T(8,128)(2,1)S(1)}, bf16[384,256]{1,0:T(8,128)(2,1)S(1)}, u32[]{:S(2)}, u32[]{:S(2)}) %collective-permute-start.47) | collective-permute-done | bytes 196640 | tf_op jit(solution)/shard_map/ppermute | solution.py:526
  299.2 3.6 collective-permute-start.50
  305.5 3.8 collective-permute-done.65
  311.3 4.9 %collective-permute-done.51 = bf16[4,24,768]{2,1,0:T(8,128)(2,1)S(1)} collective-permute-done((bf16[4,24,768]{2,1,0:T(8,128)(2,1)S(1)}, bf16[4,24,768]{2,1,0:T(8,128)(2,1)S(1)}, u32[]{:S(2)}, u32[]{:S(2)}) %collective-permute-start.51) | collective-permute-done | bytes 147488 | tf_op jit(solution)/shard_map/ppermute | solution.py:520
  320.5 20.9 %collective-permute-done.55 = bf16[2,4,24,768]{3,2,1,0:T(8,128)(2,1)S(1)} collective-permute-done((bf16[2,4,24,768]{3,2,1,0:T(8,128)(2,1)S(1)}, bf16[2,4,24,768]{3,2,1,0:T(8,128)(2,1)S(1)}, u32[]{:S(2)}, u32[]{:S(2)}) %collective-permute-start.55) | collective-permute-done | bytes 294944 | tf_op jit(solution)/shard_map/ppermute | solution.py:520
  370.3 12.3 %collective-permute-done.69 = bf16[2,4,24,2048]{3,2,1,0:T(8,128)(2,1)S(1)} collective-permute-done((bf16[2,4,24,2048]{3,2,1,0:T(8,128)(2,1)S(1)}, bf16[2,4,24,2048]{3,2,1,0:T(8,128)(2,1)S(1)}, u32[]{:S(2)}, u32[]{:S(2)}) %collective-permute-start.69) | collective-permute-done | bytes 786464 | tf_op jit(solution)/shard_map/ppermute | solution.py:520
  387.6 3.5 collective-permute-done.70
  391.2 3.8 collective-permute-done.68
  399.4 4.8 %collective-permute-done.73 = bf16[24,6912]{1,0:T(8,128)(2,1)S(1)} collective-permute-done((bf16[24,6912]{1,0:T(8,128)(2,1)S(1)}, bf16[24,6912]{1,0:T(8,128)(2,1)S(1)}, u32[]{:S(2)}, u32[]{:S(2)}) %collective-permute-start.73) | collective-permute-done | bytes 331808 | tf_op jit(solution)/shard_map/ppermute | solution.py:523
  404.2 18.1 %collective-permute-done.72 = bf16[24,6912]{1,0:T(8,128)(2,1)S(1)} collective-permute-done((bf16[24,6912]{1,0:T(8,128)(2,1)S(1)}, bf16[24,6912]{1,0:T(8,128)(2,1)S(1)}, u32[]{:S(2)}, u32[]{:S(2)}) %collective-permute-start.72) | collective-permute-done | bytes 331808 | tf_op jit(solution)/shard_map/ppermute | solution.py:523
  (396 shorter events, 150.2 us)
Async XLA Ops:
  20.3 14.1 %collective-permute-start.7 = (bf16[4,24,1152]{2,1,0:T(8,128)(2,1)S(1)}, bf16[4,24,1152]{2,1,0:T(8,128)(2,1)S(1)}, u32[]{:S(2)}, u32[]{:S(2)}) collective-permute-start(bf16[4,24,1152]{2,1,0:T(8,128)(2,1)S(1)} %constant_dynamic-slice_fusion.19), channel_id=1, source_target_pairs={{0,16},{8,24},{16,0},{24,8},{1,17},{9,25},{17,1},{25,9},{2,18},{10... | collective-permute-start | bytes 663560 | tf_op jit(solution)/shard_map/ppermute | solution.py:517
  21.8 12.1 %collective-permute-start.4 = (bf16[4,24,1280]{2,1,0:T(8,128)(2,1)S(1)}, bf16[4,24,1280]{2,1,0:T(8,128)(2,1)S(1)}, u32[]{:S(2)}, u32[]{:S(2)}) collective-permute-start(bf16[4,24,1280]{2,1,0:T(8,128)(2,1)S(1)} %constant_dynamic-slice_fusion.9), channel_id=1, source_target_pairs={{0,16},{8,24},{16,0},{24,8},{1,17},{9,25},{17,1},{25,9},{2,18},{10... | collective-permute-start | bytes 737288 | tf_op jit(solution)/shard_map/ppermute | solution.py:517
  22.3 12.0 %collective-permute-start.3 = (bf16[4,24,1280]{2,1,0:T(8,128)(2,1)S(1)}, bf16[4,24,1280]{2,1,0:T(8,128)(2,1)S(1)}, u32[]{:S(2)}, u32[]{:S(2)}) collective-permute-start(bf16[4,24,1280]{2,1,0:T(8,128)(2,1)S(1)} %constant_dynamic-slice_fusion.9), channel_id=1, source_target_pairs={{0,1},{1,0},{2,3},{3,2},{4,5},{5,4},{6,7},{7,6},{8,9},{9,8},{10,11... | collective-permute-start | bytes 737288 | tf_op jit(solution)/shard_map/ppermute | solution.py:520
  42.2 12.9 %collective-permute-start.23 = (bf16[24,6912]{1,0:T(8,128)(2,1)S(1)}, bf16[24,6912]{1,0:T(8,128)(2,1)S(1)}, u32[]{:S(2)}, u32[]{:S(2)}) collective-permute-start(bf16[24,6912]{1,0:T(8,128)(2,1)S(1)} %pad_maximum_fusion.9), channel_id=1, source_target_pairs={{0,6},{2,0},{4,2},{6,4},{1,7},{3,1},{5,3},{7,5},{8,14},{10,8},{12,... | collective-permute-start | bytes 995336 | tf_op jit(solution)/shard_map/ppermute | solution.py:523
  43.5 30.7 %collective-permute-start.24 = (bf16[24,6912]{1,0:T(8,128)(2,1)S(1)}, bf16[24,6912]{1,0:T(8,128)(2,1)S(1)}, u32[]{:S(2)}, u32[]{:S(2)}) collective-permute-start(bf16[24,6912]{1,0:T(8,128)(2,1)S(1)} %pad_maximum_fusion.9), channel_id=1, source_target_pairs={{0,4},{2,6},{4,0},{6,2},{1,5},{3,7},{5,1},{7,3},{8,12},{10,14},{12... | collective-permute-start | bytes 995336 | tf_op jit(solution)/shard_map/ppermute | solution.py:523
  44.8 29.4 %collective-permute-start.25 = (bf16[24,6912]{1,0:T(8,128)(2,1)S(1)}, bf16[24,6912]{1,0:T(8,128)(2,1)S(1)}, u32[]{:S(2)}, u32[]{:S(2)}) collective-permute-start(bf16[24,6912]{1,0:T(8,128)(2,1)S(1)} %pad_maximum_fusion.9), channel_id=1, source_target_pairs={{0,2},{2,4},{4,6},{6,0},{1,3},{3,5},{5,7},{7,1},{8,10},{10,12},{12... | collective-permute-start | bytes 995336 | tf_op jit(solution)/shard_map/ppermute | solution.py:523
  74.5 26.5 %collective-permute-start.26 = (bf16[4,24,4864]{2,1,0:T(8,128)(2,1)S(1)}, bf16[4,24,4864]{2,1,0:T(8,128)(2,1)S(1)}, u32[]{:S(2)}, u32[]{:S(2)}) collective-permute-start(bf16[4,24,4864]{2,1,0:T(8,128)(2,1)S(1)} %constant_dynamic-slice_fusion.16), channel_id=1, source_target_pairs={{0,1},{1,0},{2,3},{3,2},{4,5},{5,4},{6,7},{7,6},{8,9},{9,8},{10,11... | collective-permute-start | bytes 2801672 | tf_op jit(solution)/shard_map/ppermute | solution.py:520
  81.2 19.8 %collective-permute-start.19 = (bf16[384,256]{1,0:T(8,128)(2,1)S(1)}, bf16[384,256]{1,0:T(8,128)(2,1)S(1)}, u32[]{:S(2)}, u32[]{:S(2)}) collective-permute-start(bf16[384,256]{1,0:T(8,128)(2,1)S(1)} %collective-permute-done.15.refs_7_), channel_id=1, source_target_pairs={{0,1},{1,0},{2,3},{3,2},{4,5},{5,4},{6,7},{7,6},{8,9},{9,8},{10,11... | collective-permute-start | bytes 589832 | tf_op jit(solution)/shard_map/ppermute | solution.py:543
  82.9 22.2 %collective-permute-start.28 = (bf16[4,24,4864]{2,1,0:T(8,128)(2,1)S(1)}, bf16[4,24,4864]{2,1,0:T(8,128)(2,1)S(1)}, u32[]{:S(2)}, u32[]{:S(2)}) collective-permute-start(bf16[4,24,4864]{2,1,0:T(8,128)(2,1)S(1)} %constant_dynamic-slice_fusion.16), channel_id=1, source_target_pairs={{0,16},{8,24},{16,0},{24,8},{1,17},{9,25},{17,1},{25,9},{2,18},{10... | collective-permute-start | bytes 2801672 | tf_op jit(solution)/shard_map/ppermute | solution.py:517
  101.0 22.7 %collective-permute-start.29 = (bf16[4,24,4864]{2,1,0:T(8,128)(2,1)S(1)}, bf16[4,24,4864]{2,1,0:T(8,128)(2,1)S(1)}, u32[]{:S(2)}, u32[]{:S(2)}) collective-permute-start(bf16[4,24,4864]{2,1,0:T(8,128)(2,1)S(1)} %collective-permute-done.26), channel_id=1, source_target_pairs={{0,16},{8,24},{16,0},{24,8},{1,17},{9,25},{17,1},{25,9},{2,18},{10... | collective-permute-start | bytes 2801672 | tf_op jit(solution)/shard_map/ppermute | solution.py:517
  104.9 99.7 %collective-permute-start.27 = (bf16[192,4864]{1,0:T(8,128)(2,1)}, bf16[192,4864]{1,0:T(8,128)(2,1)}, u32[]{:S(2)}, u32[]{:S(2)}) collective-permute-start(bf16[192,4864]{1,0:T(8,128)(2,1)} %bitcast.57.refs_7_), channel_id=1, source_target_pairs={{0,8},{8,0},{16,24},{24,16},{1,9},{9,1},{17,25},{25,17},{2,10},{10... | collective-permute-start | bytes 5603336 | tf_op jit(solution)/shard_map/ppermute | solution.py:514
  124.0 80.7 %collective-permute-start.30 = (bf16[192,4864]{1,0:T(8,128)(2,1)S(1)}, bf16[192,4864]{1,0:T(8,128)(2,1)}, u32[]{:S(2)}, u32[]{:S(2)}) collective-permute-start(bf16[192,4864]{1,0:T(8,128)(2,1)S(1)} %bitcast_select_fusion.refs_9_), channel_id=1, source_target_pairs={{0,8},{8,0},{16,24},{24,16},{1,9},{9,1},{17,25},{25,17},{2,10},{10... | collective-permute-start | bytes 5603336 | tf_op jit(solution)/shard_map/ppermute | solution.py:514
  126.4 12.0 %collective-permute-start.10 = (bf16[192,256]{1,0:T(8,128)(2,1)S(1)}, bf16[192,256]{1,0:T(8,128)(2,1)S(1)}, u32[]{:S(2)}, u32[]{:S(2)}) collective-permute-start(bf16[192,256]{1,0:T(8,128)(2,1)S(1)} %get-tuple-element.200), channel_id=1, source_target_pairs={{0,2},{2,4},{4,6},{6,0},{1,3},{3,5},{5,7},{7,1},{8,10},{10,12},{12... | collective-permute-start | bytes 294920 | tf_op jit(solution)/shard_map/ppermute | solution.py:526
  135.6 17.5 %collective-permute-start.34 = (bf16[4,24,2048]{2,1,0:T(8,128)(2,1)S(1)}, bf16[4,24,2048]{2,1,0:T(8,128)(2,1)S(1)}, u32[]{:S(2)}, u32[]{:S(2)}) collective-permute-start(bf16[4,24,2048]{2,1,0:T(8,128)(2,1)S(1)} %collective-permute-done.33), channel_id=1, source_target_pairs={{0,1},{1,0},{2,3},{3,2},{4,5},{5,4},{6,7},{7,6},{8,9},{9,8},{10,11... | collective-permute-start | bytes 1179656 | tf_op jit(solution)/shard_map/ppermute | solution.py:520
  162.3 42.3 %collective-permute-start.32 = (bf16[192,2048]{1,0:T(8,128)(2,1)}, bf16[192,2048]{1,0:T(8,128)(2,1)}, u32[]{:S(2)}, u32[]{:S(2)}) collective-permute-start(bf16[192,2048]{1,0:T(8,128)(2,1)} %get-tuple-element.218.refs_11_), channel_id=1, source_target_pairs={{0,8},{8,0},{16,24},{24,16},{1,9},{9,1},{17,25},{25,17},{2,10},{10... | collective-permute-start | bytes 2359304 | tf_op jit(solution)/shard_map/ppermute | solution.py:514
  162.3 42.3 %collective-permute-start.35 = (bf16[192,2048]{1,0:T(8,128)(2,1)S(1)}, bf16[192,2048]{1,0:T(8,128)(2,1)}, u32[]{:S(2)}, u32[]{:S(2)}) collective-permute-start(bf16[192,2048]{1,0:T(8,128)(2,1)S(1)} %get-tuple-element.217.refs_13_), channel_id=1, source_target_pairs={{0,8},{8,0},{16,24},{24,16},{1,9},{9,1},{17,25},{25,17},{2,10},{10... | collective-permute-start | bytes 2359304 | tf_op jit(solution)/shard_map/ppermute | solution.py:514
  228.2 135.9 %collective-permute-start.66 = (bf16[384,4096]{1,0:T(8,128)(2,1)}, bf16[384,4096]{1,0:T(8,128)(2,1)}, u32[]{:S(2)}, u32[]{:S(2)}) collective-permute-start(bf16[384,4096]{1,0:T(8,128)(2,1)} %get-tuple-element.125), channel_id=1, source_target_pairs={{0,8},{8,0},{16,24},{24,16},{1,9},{9,1},{17,25},{25,17},{2,10},{10... | collective-permute-start | bytes 9437192 | tf_op jit(solution)/shard_map/ppermute | solution.py:514
  232.5 48.5 %collective-permute-start.63 = (bf16[384,768]{1,0:T(8,128)(2,1)}, bf16[384,768]{1,0:T(8,128)(2,1)}, u32[]{:S(2)}, u32[]{:S(2)}) collective-permute-start(bf16[384,768]{1,0:T(8,128)(2,1)} %convolution_convert_fusion.1), channel_id=1, source_target_pairs={{0,8},{8,0},{16,24},{24,16},{1,9},{9,1},{17,25},{25,17},{2,10},{10... | collective-permute-start | bytes 1769480 | tf_op jit(solution)/shard_map/ppermute | solution.py:514
  251.3 23.8 %collective-permute-start.42 = (bf16[384,256]{1,0:T(8,128)(2,1)}, bf16[384,256]{1,0:T(8,128)(2,1)S(1)}, u32[]{:S(2)}, u32[]{:S(2)}) collective-permute-start(bf16[384,256]{1,0:T(8,128)(2,1)} %get-tuple-element.103), channel_id=1, source_target_pairs={{0,1},{1,0},{2,3},{3,2},{4,5},{5,4},{6,7},{7,6},{8,9},{9,8},{10,11... | collective-permute-start | bytes 589832 | tf_op jit(solution)/shard_map/ppermute | solution.py:543
  252.3 23.6 %collective-permute-start.43 = (bf16[384,256]{1,0:T(8,128)(2,1)}, bf16[384,256]{1,0:T(8,128)(2,1)S(1)}, u32[]{:S(2)}, u32[]{:S(2)}) collective-permute-start(bf16[384,256]{1,0:T(8,128)(2,1)} %get-tuple-element.105), channel_id=1, source_target_pairs={{0,1},{1,0},{2,3},{3,2},{4,5},{5,4},{6,7},{7,6},{8,9},{9,8},{10,11... | collective-permute-start | bytes 589832 | tf_op jit(solution)/shard_map/ppermute | solution.py:543
  281.0 12.7 %collective-permute-start.47 = (bf16[384,256]{1,0:T(8,128)(2,1)S(1)}, bf16[384,256]{1,0:T(8,128)(2,1)S(1)}, u32[]{:S(2)}, u32[]{:S(2)}) collective-permute-start(bf16[384,256]{1,0:T(8,128)(2,1)S(1)} %add_convert_fusion.10), channel_id=1, source_target_pairs={{0,4},{2,6},{4,0},{6,2},{1,5},{3,7},{5,1},{7,3},{8,12},{10,14},{12... | collective-permute-start | bytes 589832 | tf_op jit(solution)/shard_map/ppermute | solution.py:526
  281.0 12.6 %collective-permute-start.49 = (bf16[384,256]{1,0:T(8,128)(2,1)S(1)}, bf16[384,256]{1,0:T(8,128)(2,1)S(1)}, u32[]{:S(2)}, u32[]{:S(2)}) collective-permute-start(bf16[384,256]{1,0:T(8,128)(2,1)S(1)} %add_convert_fusion.9), channel_id=1, source_target_pairs={{0,2},{2,4},{4,6},{6,0},{1,3},{3,5},{5,7},{7,1},{8,10},{10,12},{12... | collective-permute-start | bytes 589832 | tf_op jit(solution)/shard_map/ppermute | solution.py:526
  284.8 31.5 %collective-permute-start.60 = (bf16[384,2048]{1,0:T(8,128)(2,1)S(1)}, bf16[384,2048]{1,0:T(8,128)(2,1)S(1)}, u32[]{:S(2)}, u32[]{:S(2)}) collective-permute-start(bf16[384,2048]{1,0:T(8,128)(2,1)S(1)} %copy-done.55), channel_id=1, source_target_pairs={{0,8},{8,0},{16,24},{24,16},{1,9},{9,1},{17,25},{25,17},{2,10},{10... | collective-permute-start | bytes 4718600 | tf_op jit(solution)/shard_map/ppermute | solution.py:514
  284.8 18.3 %collective-permute-start.64 = (bf16[4,2,24,768]{3,2,0,1:T(8,128)(2,1)S(1)}, bf16[4,2,24,768]{3,2,0,1:T(8,128)(2,1)S(1)}, u32[]{:S(2)}, u32[]{:S(2)}) collective-permute-start(bf16[4,2,24,768]{3,2,0,1:T(8,128)(2,1)S(1)} %fusion.45), channel_id=1, source_target_pairs={{0,16},{8,24},{16,0},{24,8},{1,17},{9,25},{17,1},{25,9},{2,18},{10... | collective-permute-start | bytes 884744 | tf_op jit(solution)/shard_map/ppermute | solution.py:517
  299.1 17.8 %collective-permute-start.52 = (bf16[384,1536]{1,0:T(8,128)(2,1)S(1)}, bf16[384,1536]{1,0:T(8,128)(2,1)S(1)}, u32[]{:S(2)}, u32[]{:S(2)}) collective-permute-start(bf16[384,1536]{1,0:T(8,128)(2,1)S(1)} %convolution_convert_fusion), channel_id=1, source_target_pairs={{0,8},{8,0},{16,24},{24,16},{1,9},{9,1},{17,25},{25,17},{2,10},{10... | collective-permute-start | bytes 3538952 | tf_op jit(solution)/shard_map/ppermute | solution.py:514
  316.6 27.0 %collective-permute-start.61 = (bf16[2,4,24,2048]{3,2,1,0:T(8,128)(2,1)S(1)}, bf16[2,4,24,2048]{3,2,1,0:T(8,128)(2,1)S(1)}, u32[]{:S(2)}, u32[]{:S(2)}) collective-permute-start(bf16[2,4,24,2048]{3,2,1,0:T(8,128)(2,1)S(1)} %fusion.19), channel_id=1, source_target_pairs={{0,1},{1,0},{2,3},{3,2},{4,5},{5,4},{6,7},{7,6},{8,9},{9,8},{10,11... | collective-permute-start | bytes 2359304 | tf_op jit(solution)/shard_map/ppermute | solution.py:520
  317.1 24.3 %collective-permute-start.55 = (bf16[2,4,24,768]{3,2,1,0:T(8,128)(2,1)S(1)}, bf16[2,4,24,768]{3,2,1,0:T(8,128)(2,1)S(1)}, u32[]{:S(2)}, u32[]{:S(2)}) collective-permute-start(bf16[2,4,24,768]{3,2,1,0:T(8,128)(2,1)S(1)} %fusion.47), channel_id=1, source_target_pairs={{0,1},{1,0},{2,3},{3,2},{4,5},{5,4},{6,7},{7,6},{8,9},{9,8},{10,11... | collective-permute-start | bytes 884744 | tf_op jit(solution)/shard_map/ppermute | solution.py:520
  319.0 23.8 %collective-permute-start.53 = (bf16[4,2,24,768]{3,2,0,1:T(8,128)(2,1)S(1)}, bf16[4,2,24,768]{3,2,0,1:T(8,128)(2,1)S(1)}, u32[]{:S(2)}, u32[]{:S(2)}) collective-permute-start(bf16[4,2,24,768]{3,2,0,1:T(8,128)(2,1)S(1)} %fusion.43), channel_id=1, source_target_pairs={{0,16},{8,24},{16,0},{24,8},{1,17},{9,25},{17,1},{25,9},{2,18},{10... | collective-permute-start | bytes 884744 | tf_op jit(solution)/shard_map/ppermute | solution.py:517
  366.6 15.9 %collective-permute-start.69 = (bf16[2,4,24,2048]{3,2,1,0:T(8,128)(2,1)S(1)}, bf16[2,4,24,2048]{3,2,1,0:T(8,128)(2,1)S(1)}, u32[]{:S(2)}, u32[]{:S(2)}) collective-permute-start(bf16[2,4,24,2048]{3,2,1,0:T(8,128)(2,1)S(1)} %fusion.23), channel_id=1, source_target_pairs={{0,1},{1,0},{2,3},{3,2},{4,5},{5,4},{6,7},{7,6},{8,9},{9,8},{10,11... | collective-permute-start | bytes 2359304 | tf_op jit(solution)/shard_map/ppermute | solution.py:520
  368.3 18.4 %collective-permute-start.67 = (bf16[4,2,24,2048]{3,2,0,1:T(8,128)(2,1)S(1)}, bf16[4,2,24,2048]{3,2,0,1:T(8,128)(2,1)S(1)}, u32[]{:S(2)}, u32[]{:S(2)}) collective-permute-start(bf16[4,2,24,2048]{3,2,0,1:T(8,128)(2,1)S(1)} %fusion.21), channel_id=1, source_target_pairs={{0,16},{8,24},{16,0},{24,8},{1,17},{9,25},{17,1},{25,9},{2,18},{10... | collective-permute-start | bytes 2359304 | tf_op jit(solution)/shard_map/ppermute | solution.py:517
  397.1 25.2 %collective-permute-start.72 = (bf16[24,6912]{1,0:T(8,128)(2,1)S(1)}, bf16[24,6912]{1,0:T(8,128)(2,1)S(1)}, u32[]{:S(2)}, u32[]{:S(2)}) collective-permute-start(bf16[24,6912]{1,0:T(8,128)(2,1)S(1)} %get-tuple-element.155), channel_id=1, source_target_pairs={{0,4},{2,6},{4,0},{6,2},{1,5},{3,7},{5,1},{7,3},{8,12},{10,14},{12... | collective-permute-start | bytes 995336 | tf_op jit(solution)/shard_map/ppermute | solution.py:523
  397.1 25.2 %collective-permute-start.71 = (bf16[24,6912]{1,0:T(8,128)(2,1)S(1)}, bf16[24,6912]{1,0:T(8,128)(2,1)S(1)}, u32[]{:S(2)}, u32[]{:S(2)}) collective-permute-start(bf16[24,6912]{1,0:T(8,128)(2,1)S(1)} %get-tuple-element.153), channel_id=1, source_target_pairs={{0,2},{2,4},{4,6},{6,0},{1,3},{3,5},{5,7},{7,1},{8,10},{10,12},{12... | collective-permute-start | bytes 995336 | tf_op jit(solution)/shard_map/ppermute | solution.py:523
  (101 other events, 971.5 us)
